TPU v7x, 512 devices: a whole 4x8x8 slice. The times are simulated.
512 devices in a mesh: dp: 32 (over x, y_lo, core), mp: 16 (over z, y_hi).
Axes of the slice: x: 4, y: 8 (y_hi: 2, y_lo: 4; y = y_hi * 4 + y_lo), z: 8, core: 2. Of those that a mesh axis runs over, the one named last changes fastest.
Arguments:
- features: bfloat16 [57344, 1024], P(('dp', 'mp')), may hold values from -6 to 6
- row_position: int32 [57344], P(('dp', 'mp')), may hold values from 0 to 2047, as said below
- proj_weight: bfloat16 [1024, 8192], P(None, 'mp'), may hold values from -0.1875 to 0.1875
- proj_bias: float32 [8192], P('mp'), may hold values from -3 to 3
- norm_gain: float32 [8192], replicated, may hold values from 0.5 to 1.5
- cotangent: bfloat16 [65536, 8192], P(('dp', 'mp')), may hold values from -0.03125 to 0.03125
Outputs:
- grad_weight: bfloat16 [1024, 8192], P(None, 'mp')
- grad_bias: float32 [8192], P('mp')
Inputs may be any that keep to these rules, and one draw needn't show every extreme that they name: `row_position`: within each sequence's block of 1792 entries the positions are distinct; every such block holds position 0 and position 2047.
All inputs are finite; a program needn't handle non-finite values.
Results may differ from a plain program's by a relative error of at most 0.0059.
Values may be sent and summed in bfloat16 or wider, within the bound.
No kernel may reach another device: no remote copies, remote signals or barrier semaphores. Data moves between devices by JAX's collectives and lax.ppermute only.
A program may use at most 64 MiB of HBM per device.

v0:
```python
import jax
import jax.numpy as jnp
from jax import lax
from jax.sharding import PartitionSpec as P

EPSILON = 1e-05


def gelu_pair(pre_act):
    normal_cdf = 0.5 * (1.0 + lax.erf(pre_act * 0.7071067811865476))
    normal_pdf = jnp.exp(-0.5 * pre_act * pre_act) * 0.3989422804014327
    return (pre_act * normal_cdf, normal_cdf + pre_act * normal_pdf)


def per_device(features, row_position, proj_weight, proj_bias, norm_gain, cotangent):
    width = proj_weight.shape[1]
    seq_len = cotangent.shape[0] * lax.axis_size("mp")
    places = lax.all_gather(row_position, "mp", axis=0, tiled=True)
    total = places.shape[0]
    all_feats = lax.all_gather(features, "mp", axis=0, tiled=True)
    pre_act = jnp.dot(all_feats, proj_weight, preferred_element_type=jnp.float32) + proj_bias
    activated, slope = gelu_pair(pre_act)
    projected = activated.astype(jnp.bfloat16)
    source = (
        jnp.full((seq_len,), total, jnp.int32).at[places].set(jnp.arange(total, dtype=jnp.int32))
    )
    padded = jnp.concatenate([projected, jnp.zeros((1, width), jnp.bfloat16)], axis=0)
    outgoing = padded[source]
    embed = lax.all_to_all(outgoing, "mp", split_axis=0, concat_axis=1, tiled=True)
    embed_wide = lax.optimization_barrier(embed).astype(jnp.float32)
    inv_rms = lax.rsqrt(jnp.mean(embed_wide * embed_wide, axis=1, keepdims=True) + EPSILON)
    scaled_cot = cotangent.astype(jnp.float32) * norm_gain
    gdot = jnp.mean(scaled_cot * embed_wide, axis=1, keepdims=True)
    grad_embed = (inv_rms * scaled_cot - embed_wide * inv_rms * inv_rms * inv_rms * gdot).astype(
        jnp.bfloat16
    )
    returned = lax.all_to_all(grad_embed, "mp", split_axis=1, concat_axis=0, tiled=True)
    grad_proj = lax.optimization_barrier(returned[places]).astype(jnp.float32)
    grad_pre = (grad_proj * slope).astype(jnp.bfloat16)
    bias_grad = jnp.sum(grad_pre.astype(jnp.float32), axis=0)
    weight_grad = lax.dot_general(
        all_feats, grad_pre, (((0,), (0,)), ((), ())), preferred_element_type=jnp.float32
    )
    weight_grad, bias_grad = lax.psum((weight_grad, bias_grad), "dp")
    return (weight_grad.astype(jnp.bfloat16), bias_grad)


def solution(mesh):
    return jax.shard_map(
        per_device,
        mesh=mesh,
        in_specs=(
            P(("dp", "mp"), None),
            P(("dp", "mp")),
            P(None, "mp"),
            P("mp"),
            P(),
            P(("dp", "mp"), None),
        ),
        out_specs=(P(None, "mp"), P("mp")),
        check_vma=False,
    )
```

profile of v0, /device:TPU:64, one launch (start us, length us, event | category | flops | bytes accessed | tf_op | source)
XLA Modules:
  0.0 493.4 jit_solution(16986138296196837244)
XLA Ops:
  7.2 0.0 copy-start
  7.2 0.0 all-gather.2.cloned.1.call-start
  7.2 0.7 all-gather.2.cloned.1.call-update
  7.9 1.3 dynamic-slice
  9.8 0.9 dynamic-update-slice
  10.7 24.4 %all-reduce.1 = s32[1792]{0:T(1024)S(1)} all-reduce(s32[1792]{0:T(1024)S(1)} %dynamic-update-slice), channel_id=1, replica_groups=mesh['dp'=32,'mp'=16] {'mp'}, use_global_device_ids=true, to_apply=%add.1 | all-reduce | flops 1792 | bytes 14336
  35.1 7.1 %scatter_custom_fusion = s32[2048]{0:T(1024)S(1)} fusion(s32[1792]{0:T(1024)S(1)} %compare_select_fusion.1, s32[1792]{0:T(1024)S(1)} %iota.3, s32[]{:T(128)} %constant.5.clone.1), kind=kCustom, calls=%fused_computation.30 | custom fusion | bytes 8196 | tf_op jit(solution)/shard_map/scatter | solution.py:25
  42.3 98.6 %all-gather.2.cloned.1.call-done = bf16[1792,1024]{1,0:T(8,128)(2,1)} async-done(((bf16[112,1024]{1,0:T(8,128)(2,1)}), bf16[1792,1024]{1,0:T(8,128)(2,1)}) %all-gather.2.cloned.1.call-update) | async-done | bytes 3670032 | tf_op jit(solution)/shard_map/all_gather | solution.py:20
  140.9 0.0 copy-done
  140.9 5.9 %multiply_convert_fusion = (bf16[1792,512]{1,0:T(8,128)(2,1)S(1)}, f32[1792,512]{1,0:T(8,128)}) fusion(f32[512]{0:T(512)} %param.9, bf16[1792,1024]{1,0:T(8,128)(2,1)} %all-gather.2.cloned.1.call-done, bf16[1024,512]{1,0:T(8,128)(2,1)S(1)} %copy-done), kind=kOutput, calls=%fused_computation.22 | convolution fusion | flops 1884553216 | bytes 10225664 | tf_op jit(solution)/shard_map/dot_general | solution.py:21
  146.7 0.1 concatenate.3
  146.8 9.2 %gather_fusion = bf16[2048,512]{1,0:T(8,128)(2,1)} fusion(bf16[1793,512]{1,0:T(8,128)(2,1)S(1)} %concatenate.3, s32[2048]{0:T(1024)S(1)} %fusion.13), kind=kCustom, calls=%fused_computation | custom fusion | bytes 4202496 | tf_op jit(solution)/shard_map/gather | solution.py:28
  156.0 0.0 copy-start.1
  156.0 0.0 copy-start.2
  156.0 47.0 %all_to_all.38 = bf16[16,128,512]{2,1,0:T(8,128)(2,1)S(1)} all-to-all(bf16[16,128,512]{2,1,0:T(8,128)(2,1)} %bitcast.22), channel_id=1, replica_groups=mesh['dp'=32,'mp'=16] {'mp'}, dimensions={0} | all-to-all | bytes 4194304 | tf_op jit(solution)/shard_map/all_to_all | solution.py:29
  203.0 0.2 copy.12
  203.2 0.0 copy-done.1
  203.3 0.0 copy-done.2
  203.3 1.1 fusion
  204.4 1.4 fusion.5
  205.8 1.6 copy.14
  207.5 10.0 %all-to-all-start.1 = ((bf16[128,16,512]{2,0,1:T(8,128)(2,1)}), bf16[128,16,512]{2,0,1:T(8,128)(2,1)S(1)}, u32[]{:S(2)}, u32[]{:S(2)}) async-start(bf16[128,16,512]{2,0,1:T(8,128)(2,1)} %bitcast.23), calls=%async_computation.1 | async-start | bytes 4194304 | tf_op jit(solution)/shard_map/all_to_all | solution.py:37
  217.5 54.2 %all-to-all-done.1 = bf16[128,16,512]{2,0,1:T(8,128)(2,1)S(1)} async-done(((bf16[128,16,512]{2,0,1:T(8,128)(2,1)}), bf16[128,16,512]{2,0,1:T(8,128)(2,1)S(1)}, u32[]{:S(2)}, u32[]{:S(2)}) %all-to-all-start.1) | async-done | bytes 2097184 | tf_op jit(solution)/shard_map/all_to_all | solution.py:37
  271.8 0.0 copy-start.3
  271.8 6.1 %gather_fusion.1 = bf16[1792,512]{1,0:T(8,128)(2,1)} fusion(bf16[2048,512]{1,0:T(8,128)(2,1)S(1)} %bitcast.19, s32[2048]{0:T(1024)S(1)} %pad_clamp_fusion), kind=kCustom, calls=%fused_computation.1 | custom fusion | bytes 3677184 | tf_op jit(solution)/shard_map/gather | solution.py:38
  277.9 0.0 copy-done.3
  277.9 0.0 copy-start.4
  277.9 3.8 convert_reduce_fusion
  281.7 0.0 copy-done.4
  281.7 2.1 convolution_bitcast_fusion
  283.8 200.5 %all-reduce.4 = (bf16[1024,512]{0,1:T(8,128)(2,1)}, f32[512]{0:T(512)}) all-reduce(f32[1024,512]{0,1:T(8,128)S(1)} %convolution_bitcast_fusion, f32[512]{0:T(512)S(1)} %get-tuple-element.8), channel_id=1, replica_groups=mesh['dp'=32,'mp'=16] {'dp'}, use_global_device_ids=true, to_apply=%region_3.0 | all-reduce | flops 524800 | bytes 3149824 | tf_op jit(solution)/shard_map/psum | solution.py:44
  484.3 2.3 copy.10
  (6 shorter events, 0.0 us)
Async XLA Ops:
  7.2 133.7 %copy-start = (bf16[1024,512]{1,0:T(8,128)(2,1)S(1)}, bf16[1024,512]{1,0:T(8,128)(2,1)}, u32[]{:S(2)}) copy-start(bf16[1024,512]{1,0:T(8,128)(2,1)} %param.8) | copy-start | bytes 3145732
  7.2 133.7 %all-gather.2.cloned.1.call-start = ((), (), s32[]{:S(2)}) async-start(), calls=%async_computation.2 | async-start | bytes 3899392 | tf_op jit(solution)/shard_map/all_gather | solution.py:20
  156.0 47.3 %copy-start.1 = (bf16[128,8192]{1,0:T(8,128)(2,1)S(1)}, bf16[128,8192]{1,0:T(8,128)(2,1)}, u32[]{:S(2)}) copy-start(bf16[128,8192]{1,0:T(8,128)(2,1)} %param.11) | copy-start | bytes 6291460
  156.0 47.3 %copy-start.2 = (f32[8192]{0:T(1024)S(1)}, f32[8192]{0:T(1024)}, u32[]{:S(2)}) copy-start(f32[8192]{0:T(1024)} %param.10) | copy-start | bytes 98308
  207.5 64.3 %all-to-all-start.1 = ((bf16[128,16,512]{2,0,1:T(8,128)(2,1)}), bf16[128,16,512]{2,0,1:T(8,128)(2,1)S(1)}, u32[]{:S(2)}, u32[]{:S(2)}) async-start(bf16[128,16,512]{2,0,1:T(8,128)(2,1)} %bitcast.23), calls=%async_computation.1 | async-start | bytes 4194304 | tf_op jit(solution)/shard_map/all_to_all | solution.py:37
  271.8 6.1 %copy-start.3 = (f32[512]{0:T(512)S(1)}, f32[512]{0:T(512)}, u32[]{:S(2)}) copy-start(f32[512]{0:T(512)} %param.9) | copy-start | bytes 6148
  277.9 3.8 copy-start.4
Sparse Core Ops, SparseCore 0:
  11.2 129.6 all-gather.1
where the time goes:
time: 494 us; the launch traced here: 493 us
  blocking collectives  272 us (55%)
  waiting for transfers between devices  154 us (31%)
  local copies, waits for them, and re-layouts  28.8 us (6%)
  between operations  14.8 us (3%)
  starting transfers between devices  10.1 us (2%)
  matrix products  7.94 us (2%)
  other arithmetic  6.38 us (1%)
    psum x1, blocking collectives, per_device(): weight_grad, bias_grad = lax.psum((weight_grad, bias_grad), 'dp')  201 us
    all_gather x1, waiting for transfers between devices, per_device(): all_feats = lax.all_gather(features, 'mp', axis=0, tiled=True)  98.6 us
    all_to_all x1, waiting for transfers between devices, per_device(): lax.all_to_all(grad_embed, 'mp', split_axis=1, concat_axis=0, tiled=True)  54.2 us
    all_to_all x1, blocking collectives, per_device(): lax.all_to_all(outgoing, 'mp', split_axis=0, concat_axis=1, tiled=True)  47 us
    unnamed x1, blocking collectives  24.4 us
    all_to_all x1, starting transfers between devices, per_device(): lax.all_to_all(grad_embed, 'mp', split_axis=1, concat_axis=0, tiled=True)  10 us
  transfers between devices with their start and end apart: 2, of which 2 were waited for; matrix products, arithmetic and copies ran while one was open for 2% of the time, Pallas kernels for 0%

commit v1 on v0

v1 whole, which is shorter than its diff:
```python
import jax
import jax.numpy as jnp
from jax import lax
from jax.sharding import Mesh, PartitionSpec as P

EPSILON = 1e-05
DP = ("x", "yl", "c")
MP = ("z", "yh")
XY = ("x", "yl")
f32 = jnp.float32
bf16 = jnp.bfloat16


def gelu_pair(pre_act):
    normal_cdf = 0.5 * (1.0 + lax.erf(pre_act * 0.7071067811865476))
    normal_pdf = jnp.exp(-0.5 * pre_act * pre_act) * 0.3989422804014327
    return (pre_act * normal_cdf, normal_cdf + pre_act * normal_pdf)


def swap(value, axis):
    return lax.ppermute(value, axis, [(0, 1), (1, 0)])


def exchange(blocks, axes):
    return lax.all_to_all(blocks, axes, split_axis=0, concat_axis=0)


def spread(block, axes, count):
    return exchange(jnp.broadcast_to(block[None], (count,) + block.shape), axes)


def per_device(features, row_position, proj_weight, proj_bias, norm_gain, cotangent):
    rows = features.shape[0]
    vis, width = proj_weight.shape
    nz, nx, ny = lax.axis_size("z"), lax.axis_size("x"), lax.axis_size("yl")
    nm = 2 * nz
    chips = nx * ny
    seq_rows, features_out = cotangent.shape
    total = rows * nm
    z, yh, c = lax.axis_index("z"), lax.axis_index("yh"), lax.axis_index("c")
    me = z * 2 + yh

    blocks = cotangent.reshape(seq_rows, nm, width).transpose(1, 0, 2)
    cot = exchange(blocks, MP).reshape(nm * seq_rows, width)

    own = lax.all_gather(features, "z", axis=0, tiled=True)
    other = lax.all_gather(swap(features, "yh"), "z", axis=0, tiled=True)

    padded = jnp.pad(row_position, (0, 1024 - rows)).reshape(8, 128)
    places = spread(padded, MP, nm).reshape(nz, 2, 1024)[:, :, :rows]
    places = jnp.where(yh == 0, places, places[:, ::-1])
    places = places.transpose(1, 0, 2).reshape(2, nz * rows)

    gain = lax.dynamic_slice(norm_gain, (me * width,), (width,))
    halves = []
    for feats, where in ((own, places[0]), (other, places[1])):
        pre_act = jnp.dot(feats, proj_weight, preferred_element_type=f32) + proj_bias
        activated, slope = gelu_pair(pre_act)
        projected = activated.astype(bf16)
        hot = (where[:, None] == jnp.arange(nm * seq_rows)[None, :]).astype(bf16)
        picked = jnp.dot(hot, cot, preferred_element_type=f32)
        scaled = picked * gain
        wide = projected.astype(f32)
        squares = jnp.sum(wide * wide, axis=1)
        dots = jnp.sum(scaled * wide, axis=1)
        halves.append((feats, slope, wide, scaled, squares, dots))

    per_half = nz * rows
    stats = jnp.stack(
        [jnp.where(yh == 0, jnp.stack([halves[0][k], halves[1][k]]), jnp.stack([halves[1][k], halves[0][k]])) for k in (4, 5)]
    )
    stats = jnp.pad(stats.reshape(-1), (0, 4096 - 4 * per_half)).reshape(32, 128)
    stats = jnp.sum(spread(stats, MP, nm), axis=0).reshape(-1)[: 4 * per_half]
    stats = stats.reshape(2, 2, per_half) / features_out
    stats = jnp.where(yh == 0, stats, stats[:, ::-1])

    weight_grad = jnp.zeros((vis, width), f32)
    bias_grad = jnp.zeros((width,), f32)
    for k, (feats, slope, wide, scaled, _, _) in enumerate(halves):
        inv_rms = lax.rsqrt(stats[0, k] + EPSILON)[:, None]
        gdot = stats[1, k][:, None]
        grad_embed = (inv_rms * scaled - wide * (inv_rms * inv_rms * inv_rms * gdot)).astype(bf16)
        grad_pre = (grad_embed.astype(f32) * slope).astype(bf16)
        bias_grad = bias_grad + jnp.sum(grad_pre.astype(f32), axis=0)
        weight_grad = weight_grad + lax.dot_general(
            feats, grad_pre, (((0,), (0,)), ((), ())), preferred_element_type=f32
        )

    half = vis // 2
    kept = lax.dynamic_slice(weight_grad, (c * half, 0), (half, width))
    sent = lax.dynamic_slice(weight_grad, ((1 - c) * half, 0), (half, width)).astype(bf16)
    chip = (kept + swap(sent, "c").astype(f32)).astype(bf16)
    piece = exchange(chip.reshape(chips, half // chips, width), XY)
    piece = jnp.sum(piece.astype(f32), axis=0).astype(bf16)
    high = bias_grad.astype(bf16)
    low = (bias_grad - high.astype(f32)).astype(bf16)
    row = lax.broadcasted_iota(jnp.int32, (8, width), 0)
    tail = jnp.where(row == 0, high[None], jnp.where(row == 1, low[None], jnp.zeros((), bf16)))
    full = spread(jnp.concatenate([piece, tail], axis=0), XY, chips)
    mine = full[:, : half // chips].reshape(half, width)
    bias = jnp.sum(full[:, half // chips : half // chips + 2].astype(f32), axis=(0, 1))
    high = bias.astype(bf16)
    low = (bias - high.astype(f32)).astype(bf16)
    tail = jnp.where(row == 0, high[None], jnp.where(row == 1, low[None], jnp.zeros((), bf16)))
    theirs = swap(jnp.concatenate([mine, tail], axis=0), "c")
    bias = bias + jnp.sum(theirs[half : half + 2].astype(f32), axis=0)
    theirs = theirs[:half]
    first = jnp.where(c == 0, mine, theirs)
    second = jnp.where(c == 0, theirs, mine)
    return (jnp.concatenate([first, second], axis=0), bias)


def solution(mesh):
    parts = Mesh(mesh.devices.reshape(4, 4, 2, 8, 2), DP + MP)
    return jax.shard_map(
        per_device,
        mesh=parts,
        in_specs=(
            P(DP + MP, None),
            P(DP + MP),
            P(None, MP),
            P(MP),
            P(),
            P(DP + MP, None),
        ),
        out_specs=(P(None, MP), P(MP)),
        check_vma=False,
    )
```

time: 494 us -> 282 us (0.57)
  the two profiles are of different devices: /device:TPU:64 before, /device:TPU:1 now
where the time goes in v1:
time: 282 us; the launch traced here: 281 us
  waiting for transfers between devices  149 us (53%)
  starting transfers between devices  52.9 us (19%)
  blocking collectives  22.8 us (8%)
  matrix products  20.6 us (7%)
  between operations  14.4 us (5%)
  local copies, waits for them, and re-layouts  12.8 us (5%)
  other arithmetic  8.48 us (3%)
    all_gather x1, waiting for transfers between devices, per_device(): other = lax.all_gather(swap(features, 'yh'), 'z', axis=0, tiled=True)  55.6 us
    ppermute x3, waiting for transfers between devices, swap(): return lax.ppermute(value, axis, [(0, 1), (1, 0)])  37 us
    all_to_all x4, waiting for transfers between devices, exchange(): return lax.all_to_all(blocks, axes, split_axis=0, concat_axis=0)  35.7 us
    all_to_all x4, starting transfers between devices, exchange(): return lax.all_to_all(blocks, axes, split_axis=0, concat_axis=0)  34 us
    all_to_all x1, blocking collectives, exchange(): return lax.all_to_all(blocks, axes, split_axis=0, concat_axis=0)  22.8 us
    all_gather x1, waiting for transfers between devices, per_device(): own = lax.all_gather(features, 'z', axis=0, tiled=True)  20.2 us
    ppermute x3, starting transfers between devices, swap(): return lax.ppermute(value, axis, [(0, 1), (1, 0)])  18.9 us
    dot_general x2, matrix products, per_device(): picked = jnp.dot(hot, cot, preferred_element_type=f32)  9.92 us
  transfers between devices with their start and end apart: 9, of which 8 were waited for; matrix products, arithmetic and copies ran while one was open for 5% of the time, Pallas kernels for 0%

profile of v1, /device:TPU:1, one launch (start us, length us, event | category | flops | bytes accessed | tf_op | source)
XLA Modules:
  0.0 281.3 jit_solution(15657751932222950030)
XLA Ops:
  7.2 0.0 copy-start
  7.2 0.0 all-gather.3.cloned.1.call-start
  7.2 0.7 all-gather.3.cloned.1.call-update
  7.9 0.7 pad_bitcast_fusion.1
  8.6 0.6 broadcast_in_dim.64
  9.2 16.2 %all-to-all-start = ((s32[16,8,128]{2,1,0:T(8,128)}), s32[16,8,128]{2,1,0:T(8,128)S(1)}, u32[]{:S(2)}, u32[]{:S(2)}) async-start(s32[16,8,128]{2,1,0:T(8,128)} %broadcast_in_dim.64), calls=%async_computation | async-start | bytes 131072 | tf_op jit(solution)/shard_map/all_to_all | solution.py:25
  25.4 4.1 %copy.18 = bf16[128,8192]{0,1:T(8,128)(2,1)} copy(bf16[128,8192]{1,0:T(8,128)(2,1)} %param.11) | data formatting | bytes 4194304 | tf_op args[5]
  29.5 7.6 %all-to-all-done = s32[16,8,128]{2,1,0:T(8,128)S(1)} async-done(((s32[16,8,128]{2,1,0:T(8,128)}), s32[16,8,128]{2,1,0:T(8,128)S(1)}, u32[]{:S(2)}, u32[]{:S(2)}) %all-to-all-start) | async-done | bytes 65568 | tf_op jit(solution)/shard_map/all_to_all | solution.py:25
  37.2 0.0 copy-start.6
  37.2 4.0 %all-to-all-start.1 = ((bf16[16,128,512]{1,2,0:T(8,128)(2,1)}), bf16[16,128,512]{1,2,0:T(8,128)(2,1)S(1)}, u32[]{:S(2)}, u32[]{:S(2)}) async-start(bf16[16,128,512]{1,2,0:T(8,128)(2,1)} %bitcast.3), calls=%async_computation.1 | async-start | bytes 4194304 | tf_op jit(solution)/shard_map/all_to_all | solution.py:25
  41.2 0.0 all-gather.5.cloned.1.call-start
  41.2 0.0 copy-done.6
  41.2 7.2 %collective-permute-start = (bf16[112,1024]{1,0:T(8,128)(2,1)S(1)}, bf16[112,1024]{1,0:T(8,128)(2,1)}, u32[]{:S(2)}, u32[]{:S(2)}) collective-permute-start(bf16[112,1024]{1,0:T(8,128)(2,1)S(1)} %copy-done.6), channel_id=1, source_target_pairs={{0,1},{1,0},{2,3},{3,2},{4,5},{5,4},{6,7},{7,6},{8,9},{9,8},{10,11... | collective-permute-start | bytes 688136 | tf_op jit(solution)/shard_map/ppermute | solution.py:21
  48.4 34.0 %collective-permute-done = bf16[112,1024]{1,0:T(8,128)(2,1)} collective-permute-done((bf16[112,1024]{1,0:T(8,128)(2,1)S(1)}, bf16[112,1024]{1,0:T(8,128)(2,1)}, u32[]{:S(2)}, u32[]{:S(2)}) %collective-permute-start) | collective-permute-done | bytes 229408 | tf_op jit(solution)/shard_map/ppermute | solution.py:21
  82.4 0.0 all-gather.5.cloned.1.call-update
  82.4 0.8 dynamic_slice.9
  83.3 0.1 eq.60
  83.4 0.1 eq.56
  83.4 20.2 %all-gather.3.cloned.1.call-done = bf16[896,1024]{1,0:T(8,128)(2,1)} async-done(((bf16[112,1024]{1,0:T(8,128)(2,1)}), bf16[896,1024]{1,0:T(8,128)(2,1)}) %all-gather.3.cloned.1.call-update) | async-done | bytes 1835024 | tf_op jit(solution)/shard_map/all_gather | solution.py:46
  103.7 0.0 copy-done
  103.7 4.1 %fusion.34 = f32[896,512]{0,1:T(8,128)} fusion(bf16[896,1024]{1,0:T(8,128)(2,1)} %all-gather.3.cloned.1.call-done, bf16[1024,512]{1,0:T(8,128)(2,1)S(1)} %copy-done), kind=kOutput, calls=%fused_computation.80 | convolution fusion | flops 939524096 | bytes 4718592 | tf_op jit(solution)/shard_map/dot_general | solution.py:57
  107.8 55.6 %all-gather.5.cloned.1.call-done = bf16[896,1024]{1,0:T(8,128)(2,1)} async-done(((bf16[112,1024]{1,0:T(8,128)(2,1)}), bf16[896,1024]{1,0:T(8,128)(2,1)}) %all-gather.5.cloned.1.call-update) | async-done | bytes 1835024 | tf_op jit(solution)/shard_map/all_gather | solution.py:47
  163.4 4.0 %fusion.35 = f32[896,512]{0,1:T(8,128)} fusion(bf16[896,1024]{1,0:T(8,128)(2,1)} %all-gather.5.cloned.1.call-done, bf16[1024,512]{1,0:T(8,128)(2,1)S(1)} %copy-done), kind=kOutput, calls=%fused_computation.81 | convolution fusion | flops 939524096 | bytes 4718592 | tf_op jit(solution)/shard_map/dot_general | solution.py:57
  167.5 0.0 all-to-all-done.1
  167.5 2.6 copy.19
  170.1 0.0 copy-start.1
  170.1 0.0 copy-start.2
  170.1 4.3 %fusion.1 = f32[896,512]{0,1:T(8,128)S(1)} fusion(bf16[2048,512]{1,0:T(8,128)(2,1)} %bitcast.32, s32[896]{0:T(1024)S(1)} %eq.60), kind=kOutput, calls=%fused_computation.3 | convolution fusion | flops 1880883200 | bytes 3935744 | tf_op jit(solution)/shard_map/dot_general | solution.py:61
  174.4 0.0 copy-done.1
  174.4 0.0 copy-done.2
  174.4 0.0 copy-done.3
  174.5 0.0 copy-done.7
  174.5 0.0 copy-start.4
  174.5 5.6 %fusion.4 = (f32[896]{0:T(1024)S(1)}, f32[896]{0:T(1024)S(1)}, bf16[896,512]{0,1:T(8,128)(2,1)}, f32[896]{0:T(1024)S(1)}, f32[896]{0:T(1024)S(1)}, /*index=5*/bf16[896,512]{0,1:T(8,128)(2,1)}, f32[896,512]{0,1:T(8,128)}) fusion(f32[512]{0:T(512)S(1)} %dynamic_slice.9, f32[896,512]{0,1:T(8,128)S(1)} %copy-done.2, f32[512]{0:T(512)S(1)} %copy-done.7, ...), kind=kOutput, calls=%fused_computation.14 | convolution fusion | flops 1891889664 | bytes 11294208 | tf_op jit(solution)/shard_map/dot_general | solution.py:61
  180.1 0.0 copy-done.4
  180.2 0.7 broadcast_in_dim.66
  180.9 8.8 %all-to-all-start.2 = ((f32[16,32,128]{2,1,0:T(8,128)}), f32[16,32,128]{2,1,0:T(8,128)S(1)}, u32[]{:S(2)}, u32[]{:S(2)}) async-start(f32[16,32,128]{2,1,0:T(8,128)} %broadcast_in_dim.66), calls=%async_computation.2 | async-start | bytes 524288 | tf_op jit(solution)/shard_map/all_to_all | solution.py:25
  189.7 12.5 %all-to-all-done.2 = f32[16,32,128]{2,1,0:T(8,128)S(1)} async-done(((f32[16,32,128]{2,1,0:T(8,128)}), f32[16,32,128]{2,1,0:T(8,128)S(1)}, u32[]{:S(2)}, u32[]{:S(2)}) %all-to-all-start.2) | async-done | bytes 262176 | tf_op jit(solution)/shard_map/all_to_all | solution.py:25
  202.2 0.2 reverse.3
  202.5 0.0 copy-start.8
  202.6 4.9 %convert_reduce_fusion = (f32[512]{0:T(512)S(1)}, bf16[896,512]{0,1:T(8,128)(2,1)S(1)}, f32[512]{0:T(512)S(1)}, bf16[896,512]{0,1:T(8,128)(2,1)S(1)}) fusion(f32[896,512]{0,1:T(8,128)} %fusion.35, f32[512]{0:T(512)S(1)} %copy-done.7, f32[896]{0:T(1024)S(1)} %fusion.27, bf16[896,512]{0,1:T(8,128)(2,1)} %get-tuple-element.28, f32[896,512]{0,1:T(8,128)} %copy-done.4, ...), kind=kLoop, calls=%fused_computation.34 | loop fusion | flops 18349056 | bytes 11032576 | tf_op jit(solution)/shard_map/reduce_sum | solution.py:84
  207.4 0.0 copy-done.8
  207.4 0.0 copy-start.9
  207.4 1.2 fusion.36
  208.7 0.2 copy-done.9
  208.9 1.3 convolution_add_fusion
  210.2 0.0 copy-start.5
  210.2 1.3 copy-done.5
  211.6 0.1 fusion.25
  211.7 8.4 %collective-permute-start.1 = (bf16[512,512]{0,1:T(8,128)(2,1)S(1)}, bf16[512,512]{0,1:T(8,128)(2,1)S(1)}, u32[]{:S(2)}, u32[]{:S(2)}) collective-permute-start(bf16[512,512]{0,1:T(8,128)(2,1)S(1)} %fusion.25), channel_id=1, source_target_pairs={{0,16},{16,0},{1,17},{17,1},{2,18},{18,2},{3,19},{19,3},{4,20},{20... | collective-permute-start | bytes 1572872 | tf_op jit(solution)/shard_map/ppermute | solution.py:21
  220.1 1.5 collective-permute-done.1
  221.6 1.4 fusion.24
  223.0 1.0 copy.22
  224.0 5.0 %all-to-all-start.3 = ((bf16[16,32,512]{2,1,0:T(8,128)(2,1)}), bf16[16,32,512]{2,1,0:T(8,128)(2,1)S(1)}, u32[]{:S(2)}, u32[]{:S(2)}) async-start(bf16[16,32,512]{2,1,0:T(8,128)(2,1)} %bitcast.8), calls=%async_computation.3 | async-start | bytes 1048576 | tf_op jit(solution)/shard_map/all_to_all | solution.py:25
  229.0 0.1 select_select_fusion.1
  229.1 15.7 %all-to-all-done.3 = bf16[16,32,512]{2,1,0:T(8,128)(2,1)S(1)} async-done(((bf16[16,32,512]{2,1,0:T(8,128)(2,1)}), bf16[16,32,512]{2,1,0:T(8,128)(2,1)S(1)}, u32[]{:S(2)}, u32[]{:S(2)}) %all-to-all-start.3) | async-done | bytes 524320 | tf_op jit(solution)/shard_map/all_to_all | solution.py:25
  244.8 0.1 reduce_sum.98
  244.9 22.8 %all_to_all.25 = bf16[16,40,512]{2,1,0:T(8,128)(2,1)S(1)} all-to-all(bf16[16,40,512]{2,1,0:T(8,128)(2,1)S(1)} %broadcast_in_dim.70), channel_id=1, replica_groups=mesh['x'=4,'yl'=4,'c'=2,'z'=8,'yh'=2] {'x','yl'}, dimensions={0} | all-to-all | bytes 1310720 | tf_op jit(solution)/shard_map/all_to_all | solution.py:25
  267.7 0.1 select_select_fusion
  267.9 3.3 %collective-permute-start.2 = (bf16[520,512]{1,0:T(8,128)(2,1)S(1)}, bf16[520,512]{1,0:T(8,128)(2,1)S(1)}, u32[]{:S(2)}, u32[]{:S(2)}) collective-permute-start(bf16[520,512]{1,0:T(8,128)(2,1)S(1)} %pad_maximum_fusion.1), channel_id=1, source_target_pairs={{0,16},{16,0},{1,17},{17,1},{2,18},{18,2},{3,19},{19,3},{4,20},{20... | collective-permute-start | bytes 1597448 | tf_op jit(solution)/shard_map/ppermute | solution.py:21
  271.2 1.5 collective-permute-done.2
  272.8 0.6 add.100
  273.3 0.1 broadcast_select_fusion.1
  273.4 1.0 pad_maximum_fusion
  (30 shorter events, 0.5 us)
Async XLA Ops:
  7.2 96.5 %copy-start = (bf16[1024,512]{1,0:T(8,128)(2,1)S(1)}, bf16[1024,512]{1,0:T(8,128)(2,1)}, u32[]{:S(2)}) copy-start(bf16[1024,512]{1,0:T(8,128)(2,1)} %param.8) | copy-start | bytes 3145732
  7.2 96.5 %all-gather.3.cloned.1.call-start = ((), (), s32[]{:S(2)}) async-start(), calls=%async_computation.5 | async-start | bytes 2064384 | tf_op jit(solution)/shard_map/all_gather | solution.py:46
  9.2 28.0 %all-to-all-start = ((s32[16,8,128]{2,1,0:T(8,128)}), s32[16,8,128]{2,1,0:T(8,128)S(1)}, u32[]{:S(2)}, u32[]{:S(2)}) async-start(s32[16,8,128]{2,1,0:T(8,128)} %broadcast_in_dim.64), calls=%async_computation | async-start | bytes 131072 | tf_op jit(solution)/shard_map/all_to_all | solution.py:25
  37.2 4.0 %copy-start.6 = (bf16[112,1024]{1,0:T(8,128)(2,1)S(1)}, bf16[112,1024]{1,0:T(8,128)(2,1)}, u32[]{:S(2)}) copy-start(bf16[112,1024]{1,0:T(8,128)(2,1)} %param.6) | copy-start | bytes 688132
  37.2 130.3 %all-to-all-start.1 = ((bf16[16,128,512]{1,2,0:T(8,128)(2,1)}), bf16[16,128,512]{1,2,0:T(8,128)(2,1)S(1)}, u32[]{:S(2)}, u32[]{:S(2)}) async-start(bf16[16,128,512]{1,2,0:T(8,128)(2,1)} %bitcast.3), calls=%async_computation.1 | async-start | bytes 4194304 | tf_op jit(solution)/shard_map/all_to_all | solution.py:25
  41.2 122.3 %all-gather.5.cloned.1.call-start = ((), (), s32[]{:S(2)}) async-start(), calls=%async_computation.6 | async-start | bytes 2064384 | tf_op jit(solution)/shard_map/all_gather | solution.py:47
  41.2 41.2 %collective-permute-start = (bf16[112,1024]{1,0:T(8,128)(2,1)S(1)}, bf16[112,1024]{1,0:T(8,128)(2,1)}, u32[]{:S(2)}, u32[]{:S(2)}) collective-permute-start(bf16[112,1024]{1,0:T(8,128)(2,1)S(1)} %copy-done.6), channel_id=1, source_target_pairs={{0,1},{1,0},{2,3},{3,2},{4,5},{5,4},{6,7},{7,6},{8,9},{9,8},{10,11... | collective-permute-start | bytes 688136 | tf_op jit(solution)/shard_map/ppermute | solution.py:21
  170.1 4.4 %copy-start.1 = (bf16[16,128,512]{2,1,0:T(8,128)(2,1)S(1)}, bf16[16,128,512]{2,1,0:T(8,128)(2,1)}, u32[]{:S(2)}) copy-start(bf16[16,128,512]{2,1,0:T(8,128)(2,1)} %copy.19) | copy-start | bytes 6291460
  170.1 4.4 %copy-start.2 = (f32[896,512]{0,1:T(8,128)S(1)}, f32[896,512]{0,1:T(8,128)}, u32[]{:S(2)}) copy-start(f32[896,512]{0,1:T(8,128)} %fusion.34) | copy-start | bytes 5505028
  170.1 4.4 %copy-start.3 = (f32[896,512]{0,1:T(8,128)S(1)}, f32[896,512]{0,1:T(8,128)}, u32[]{:S(2)}) copy-start(f32[896,512]{0,1:T(8,128)} %fusion.35) | copy-start | bytes 5505028
  170.1 4.4 %copy-start.7 = (f32[512]{0:T(512)S(1)}, f32[512]{0:T(512)}, u32[]{:S(2)}) copy-start(f32[512]{0:T(512)} %param.9) | copy-start | bytes 6148
  174.5 5.6 %copy-start.4 = (f32[896,512]{0,1:T(8,128)}, f32[896,512]{0,1:T(8,128)S(1)}, u32[]{:S(2)}) copy-start(f32[896,512]{0,1:T(8,128)S(1)} %fusion.1) | copy-start | bytes 5505028
  180.9 21.3 %all-to-all-start.2 = ((f32[16,32,128]{2,1,0:T(8,128)}), f32[16,32,128]{2,1,0:T(8,128)S(1)}, u32[]{:S(2)}, u32[]{:S(2)}) async-start(f32[16,32,128]{2,1,0:T(8,128)} %broadcast_in_dim.66), calls=%async_computation.2 | async-start | bytes 524288 | tf_op jit(solution)/shard_map/all_to_all | solution.py:25
  202.5 4.9 %copy-start.8 = (bf16[896,1024]{1,0:T(8,128)(2,1)S(1)}, bf16[896,1024]{1,0:T(8,128)(2,1)}, u32[]{:S(2)}) copy-start(bf16[896,1024]{1,0:T(8,128)(2,1)} %all-gather.3.cloned.1.call-done) | copy-start | bytes 5505028
  207.4 1.5 copy-start.9
  210.2 1.4 copy-start.5
  211.7 9.9 %collective-permute-start.1 = (bf16[512,512]{0,1:T(8,128)(2,1)S(1)}, bf16[512,512]{0,1:T(8,128)(2,1)S(1)}, u32[]{:S(2)}, u32[]{:S(2)}) collective-permute-start(bf16[512,512]{0,1:T(8,128)(2,1)S(1)} %fusion.25), channel_id=1, source_target_pairs={{0,16},{16,0},{1,17},{17,1},{2,18},{18,2},{3,19},{19,3},{4,20},{20... | collective-permute-start | bytes 1572872 | tf_op jit(solution)/shard_map/ppermute | solution.py:21
  224.0 20.8 %all-to-all-start.3 = ((bf16[16,32,512]{2,1,0:T(8,128)(2,1)}), bf16[16,32,512]{2,1,0:T(8,128)(2,1)S(1)}, u32[]{:S(2)}, u32[]{:S(2)}) async-start(bf16[16,32,512]{2,1,0:T(8,128)(2,1)} %bitcast.8), calls=%async_computation.3 | async-start | bytes 1048576 | tf_op jit(solution)/shard_map/all_to_all | solution.py:25
  267.9 4.8 %collective-permute-start.2 = (bf16[520,512]{1,0:T(8,128)(2,1)S(1)}, bf16[520,512]{1,0:T(8,128)(2,1)S(1)}, u32[]{:S(2)}, u32[]{:S(2)}) collective-permute-start(bf16[520,512]{1,0:T(8,128)(2,1)S(1)} %pad_maximum_fusion.1), channel_id=1, source_target_pairs={{0,16},{16,0},{1,17},{17,1},{2,18},{18,2},{3,19},{19,3},{4,20},{20... | collective-permute-start | bytes 1597448 | tf_op jit(solution)/shard_map/ppermute | solution.py:21
Sparse Core Ops, SparseCore 0:
  10.1 93.5 all-gather.2
  105.7 57.6 all-gather.4

commit v2 on v0

v2 whole, which is shorter than its diff:
```python
import functools

import jax
import jax.numpy as jnp
from jax import lax
from jax.experimental import pallas as pl
from jax.experimental.pallas import tpu as pltpu
from jax.sharding import Mesh, PartitionSpec as P


EPSILON = 1e-05
DP = ("x", "yl", "c")
MP = ("z", "yh")
XY = ("x", "yl")
f32 = jnp.float32
bf16 = jnp.bfloat16
TILE = 256
LANES = 128
EARLY = 32
HEAD = 8
MIB = 1024 * 1024


def swap(value, axis):
    return lax.ppermute(value, axis, [(0, 1), (1, 0)])


def exchange(blocks, axes):
    return lax.all_to_all(blocks, axes, split_axis=0, concat_axis=0)


def spread(block, axes, count):
    return exchange(jnp.broadcast_to(block[None], (count,) + block.shape), axes)


def params(mib):
    return pltpu.CompilerParams(vmem_limit_bytes=mib * MIB)


def pick_kernel(index_ref, early_ref, late_ref, picked_ref):
    index = index_ref[...]
    total = jnp.zeros(picked_ref.shape, f32)
    start = 0
    for source in (early_ref, late_ref):
        depth = source.shape[0]
        columns = lax.broadcasted_iota(jnp.int32, (index.shape[0], depth), 1) + start
        hot = jnp.where(columns == index, 1.0, 0.0).astype(bf16)
        total = total + jnp.dot(hot, source[...], preferred_element_type=f32)
        start += depth
    picked_ref[...] = total.astype(bf16)


def pick(index, early, late):
    total, width = index.shape[0], early.shape[1]
    return pl.pallas_call(
        pick_kernel,
        grid=(total // TILE,),
        in_specs=[
            pl.BlockSpec((TILE, 1), lambda i: (i, 0)),
            pl.BlockSpec(early.shape, lambda i: (0, 0)),
            pl.BlockSpec(late.shape, lambda i: (0, 0)),
        ],
        out_specs=pl.BlockSpec((TILE, width), lambda i: (i, 0)),
        out_shape=jax.ShapeDtypeStruct((total, width), bf16),
        compiler_params=params(16),
        cost_estimate=pl.CostEstimate(
            flops=2 * total * (early.shape[0] + late.shape[0]) * width, bytes_accessed=6 << 20, transcendentals=0
        ),
        name="pick",
    )(index, early, late)


def project_kernel(feats_ref, weight_ref, bias_ref, gain_ref, picked_ref, proj_ref, slope_ref, stats_ref):
    step = pl.program_id(0)
    value = jnp.dot(feats_ref[...], weight_ref[...], preferred_element_type=f32) + bias_ref[...]
    cdf = 0.5 * (1.0 + lax.erf(value * 0.7071067811865476))
    pdf = jnp.exp(-0.5 * value * value) * 0.3989422804014327
    slope_ref[...] = cdf + value * pdf
    projected = (value * cdf).astype(bf16)
    proj_ref[...] = projected
    wide = projected.astype(f32)
    squares = jnp.sum(wide * wide, axis=1, keepdims=True)
    dots = jnp.sum(picked_ref[...].astype(f32) * gain_ref[...] * wide, axis=1, keepdims=True)

    @pl.when(step == 0)
    def _():
        stats_ref[...] = jnp.zeros_like(stats_ref)

    lane = lax.broadcasted_iota(jnp.int32, (LANES, LANES), 1)
    parts = TILE // LANES
    for part in range(parts):
        rows = slice(part * LANES, (part + 1) * LANES)
        both = jnp.where(lane == 0, squares[rows], dots[rows]).T
        row = step * parts + part
        stats_ref[pl.ds(row, 1), :] = both[0:1]
        stats_ref[pl.ds(stats_ref.shape[0] // 2 + row, 1), :] = both[1:2]


def project(feats, weight, bias, gain, picked):
    total, vis = feats.shape
    width = weight.shape[1]
    stat_rows = 2 * (-(-total // LANES // 8) * 8)
    return pl.pallas_call(
        project_kernel,
        grid=(total // TILE,),
        in_specs=[
            pl.BlockSpec((TILE, vis), lambda i: (i, 0)),
            pl.BlockSpec((vis, width), lambda i: (0, 0)),
            pl.BlockSpec((1, width), lambda i: (0, 0)),
            pl.BlockSpec((1, width), lambda i: (0, 0)),
            pl.BlockSpec((TILE, width), lambda i: (i, 0)),
        ],
        out_specs=[
            pl.BlockSpec((TILE, width), lambda i: (i, 0)),
            pl.BlockSpec((TILE, width), lambda i: (i, 0)),
            pl.BlockSpec((stat_rows, LANES), lambda i: (0, 0)),
        ],
        out_shape=[
            jax.ShapeDtypeStruct((total, width), bf16),
            jax.ShapeDtypeStruct((total, width), f32),
            jax.ShapeDtypeStruct((stat_rows, LANES), f32),
        ],
        compiler_params=params(61),
        cost_estimate=pl.CostEstimate(flops=2 * total * vis * width, bytes_accessed=10 << 20, transcendentals=total * width),
        name="project",
    )(feats, weight, bias, gain, picked)


def backward_kernel(
    core_ref, feats_ref, gain_ref, picked_ref, proj_ref, slope_ref, stats_ref, sent_ref, kept_ref, bias_ref, acc, bias_acc, sums,
    *, features_out, pieces
):
    step = pl.program_id(0)

    @pl.when(step == 0)
    def _():
        acc[...] = jnp.zeros_like(acc)
        bias_acc[...] = jnp.zeros_like(bias_acc)
        means = jnp.sum(stats_ref[...], axis=0) / features_out
        half = means.shape[0] // 2
        inv_rms = lax.rsqrt(means[:half] + EPSILON)
        sums[:half] = inv_rms
        sums[half:] = inv_rms * inv_rms * inv_rms * means[half:]

    parts = TILE // LANES
    half = sums.shape[0] // 2
    width = proj_ref.shape[1]
    grads = []
    for part in range(parts):
        rows = slice(part * LANES, (part + 1) * LANES)
        row = step * parts + part
        inv_rms = jnp.broadcast_to(sums[pl.ds(row, 1), :], (LANES, LANES)).T
        factor = jnp.broadcast_to(sums[pl.ds(half + row, 1), :], (LANES, LANES)).T
        columns = []
        for j in range(width // LANES):
            cols = slice(j * LANES, (j + 1) * LANES)
            scaled = picked_ref[rows, cols].astype(f32) * gain_ref[:, cols]
            grad = (inv_rms * scaled - proj_ref[rows, cols].astype(f32) * factor).astype(bf16)
            columns.append((grad.astype(f32) * slope_ref[rows, cols]).astype(bf16))
        grads.append(jnp.concatenate(columns, axis=1))
    grad_pre = jnp.concatenate(grads, axis=0)
    bias_acc[...] += jnp.sum(grad_pre.astype(f32).reshape(TILE // 8, 8, width), axis=0)
    acc[...] += lax.dot_general(feats_ref[...], grad_pre, (((0,), (0,)), ((), ())), preferred_element_type=f32)

    @pl.when(step == pl.num_programs(0) - 1)
    def _():
        vis = acc.shape[0]
        rows = vis // 2 // pieces
        core = core_ref[0]
        for piece in range(pieces):
            for j in range(width // LANES):
                cols = slice(j * LANES, (j + 1) * LANES)
                at = (piece * (width // LANES) + j) * rows
                mine = pl.multiple_of(core * (vis // 2) + piece * rows, 8)
                other = pl.multiple_of((1 - core) * (vis // 2) + piece * rows, 8)
                kept_ref[at : at + rows, :] = acc[pl.ds(mine, rows), cols]
                sent_ref[at : at + rows, :] = acc[pl.ds(other, rows), cols].astype(bf16)
        bias = jnp.sum(bias_acc[...], axis=0, keepdims=True)
        lines = jnp.concatenate([bias[:, j * LANES : (j + 1) * LANES] for j in range(width // LANES)], axis=0)
        bias_ref[...] = lines
        high = lines.astype(bf16).astype(f32)
        both = jnp.concatenate([high, lines - high], axis=0).astype(bf16)
        sent_ref[sent_ref.shape[0] - 2 * lines.shape[0] :, :] = both


def backward(core, feats, gain, picked, proj, slope, stats, features_out, pieces):
    total, vis = feats.shape
    width = proj.shape[1]
    lines = width // LANES
    out_rows = vis // 2 * lines
    return pl.pallas_call(
        functools.partial(backward_kernel, features_out=features_out, pieces=pieces),
        grid_spec=pltpu.PrefetchScalarGridSpec(
            num_scalar_prefetch=1,
            grid=(total // TILE,),
            in_specs=[
                pl.BlockSpec((TILE, vis), lambda i, c: (i, 0)),
                pl.BlockSpec((1, width), lambda i, c: (0, 0)),
                pl.BlockSpec((TILE, width), lambda i, c: (i, 0)),
                pl.BlockSpec((TILE, width), lambda i, c: (i, 0)),
                pl.BlockSpec((TILE, width), lambda i, c: (i, 0)),
                pl.BlockSpec(stats.shape, lambda i, c: (0, 0, 0)),
            ],
            out_specs=[
                pl.BlockSpec((out_rows + 2 * lines, LANES), lambda i, c: (0, 0)),
                pl.BlockSpec((out_rows, LANES), lambda i, c: (0, 0)),
                pl.BlockSpec((lines, LANES), lambda i, c: (0, 0)),
            ],
            scratch_shapes=[
                pltpu.VMEM((vis, width), f32),
                pltpu.VMEM((8, width), f32),
                pltpu.VMEM(stats.shape[1:], f32),
            ],
        ),
        out_shape=[
            jax.ShapeDtypeStruct((out_rows + 2 * lines, LANES), bf16),
            jax.ShapeDtypeStruct((out_rows, LANES), f32),
            jax.ShapeDtypeStruct((lines, LANES), f32),
        ],
        compiler_params=params(61),
        cost_estimate=pl.CostEstimate(flops=2 * total * vis * width, bytes_accessed=10 << 20, transcendentals=0),
        name="backward",
    )(core, feats, gain, picked, proj, slope, stats)


def assemble_kernel(core_ref, mine_ref, theirs_ref, grad_ref, bias_ref, *, size):
    core = core_ref[0]
    pieces = mine_ref.shape[0]
    vis, width = grad_ref.shape
    lines = width // LANES
    rows = size // lines
    for piece in range(pieces):
        for j in range(lines):
            cols = slice(j * LANES, (j + 1) * LANES)
            part = slice(j * rows, (j + 1) * rows)
            for half, ref in ((core, mine_ref), (1 - core, theirs_ref)):
                at = pl.multiple_of(half * (vis // 2) + piece * rows, rows)
                grad_ref[pl.ds(at, rows), cols] = ref[piece, part, :]
    both = jnp.sum(mine_ref[:, size:, :].astype(f32), axis=0)
    bias_ref[...] = both[:lines] + both[lines:]


def assemble(core, mine, theirs, vis, width, size):
    return pl.pallas_call(
        functools.partial(assemble_kernel, size=size),
        in_specs=[
            pl.BlockSpec(memory_space=pltpu.SMEM),
            pl.BlockSpec(memory_space=pltpu.VMEM),
            pl.BlockSpec(memory_space=pltpu.VMEM),
        ],
        out_specs=[pl.BlockSpec(memory_space=pltpu.VMEM), pl.BlockSpec(memory_space=pltpu.VMEM)],
        out_shape=[jax.ShapeDtypeStruct((vis, width), bf16), jax.ShapeDtypeStruct((width // LANES, LANES), f32)],
        compiler_params=params(8),
        cost_estimate=pl.CostEstimate(flops=0, bytes_accessed=2 << 20, transcendentals=0),
        name="assemble",
    )(core, mine, theirs)


def per_device(features, row_position, proj_weight, proj_bias, norm_gain, cotangent):
    rows = features.shape[0]
    vis, width = proj_weight.shape
    nz, nx, ny = lax.axis_size("z"), lax.axis_size("x"), lax.axis_size("yl")
    nm = 2 * nz
    chips = nx * ny
    seq_rows, features_out = cotangent.shape
    total = rows * nm
    z, yh, c = lax.axis_index("z"), lax.axis_index("yh"), lax.axis_index("c")
    me = z * 2 + yh
    partner = swap(features, "yh")
    digits = jnp.stack([row_position // LANES, row_position % LANES]).astype(bf16)
    digits = jnp.pad(digits, ((0, HEAD - 2), (0, width - rows)))
    blocks = cotangent.reshape(seq_rows, nm, width)
    early = jnp.concatenate([jnp.broadcast_to(digits[:, None], (HEAD, nm, width)), blocks[:EARLY]], axis=0)
    early = exchange(early.transpose(1, 0, 2), MP)
    pair = jnp.concatenate([features, partner], axis=0)
    pair = jnp.where(yh == 0, pair, jnp.concatenate([partner, features], axis=0))
    pair, late = lax.optimization_barrier((pair, blocks[EARLY:].transpose(1, 0, 2)))
    feats = lax.all_gather(pair, "z", axis=0, tiled=True)
    late = exchange(late, MP)

    digits = early[:, :2, :rows].astype(jnp.int32)
    places = (digits[:, 0] * LANES + digits[:, 1]).reshape(total, 1)
    owner, offset = places // seq_rows, places % seq_rows
    index = jnp.where(
        offset < EARLY,
        owner * (HEAD + EARLY) + HEAD + offset,
        nm * (HEAD + EARLY) + owner * (seq_rows - EARLY) + offset - EARLY,
    )
    picked = pick(index, early.reshape(-1, width), late.reshape(-1, width))

    gain = lax.dynamic_slice(norm_gain, (me * width,), (width,))[None]
    proj, slope, stats = project(feats, proj_weight, proj_bias[None], gain, picked)
    stats = spread(stats, MP, nm)
    core = c.astype(jnp.int32)[None]
    sent, kept, bias = backward(core, feats, gain, picked, proj, slope, stats, features_out, chips)

    lines = width // LANES
    got = swap(sent, "c")
    size = kept.shape[0]
    chip = (kept + got[:size].astype(f32)).astype(bf16)
    bias = bias + got[size : size + lines].astype(f32) + got[size + lines :].astype(f32)
    piece = exchange(chip.reshape(chips, size // chips, LANES), XY)
    piece = jnp.sum(piece.astype(f32), axis=0).astype(bf16)
    high = bias.astype(bf16)
    low = (bias - high.astype(f32)).astype(bf16)
    full = spread(jnp.concatenate([piece, high, low], axis=0), XY, chips)
    theirs = swap(full, "c")
    grad, bias = assemble(core, full, theirs, vis, width, size // chips)
    return (grad, bias.reshape(width))


def solution(mesh):
    parts = Mesh(mesh.devices.reshape(4, 4, 2, 8, 2), DP + MP)
    return jax.shard_map(
        per_device,
        mesh=parts,
        in_specs=(P(DP + MP, None), P(DP + MP), P(None, MP), P(MP), P(), P(DP + MP, None)),
        out_specs=(P(None, MP), P(MP)),
        check_vma=False,
    )
```

time: 494 us -> 244 us (0.49)
  the two profiles are of different devices: /device:TPU:64 before, /device:TPU:1 now
where the time goes in v2:
time: 244 us; the launch traced here: 243 us
  waiting for transfers between devices  90.2 us (37%)
  starting transfers between devices  49.1 us (20%)
  blocking collectives  49.1 us (20%)
  Pallas kernels  26.5 us (11%)
  between operations  14.2 us (6%)
  local copies, waits for them, and re-layouts  7.98 us (3%)
  other arithmetic  5.46 us (2%)
    all_to_all x3, waiting for transfers between devices, exchange(): return lax.all_to_all(blocks, axes, split_axis=0, concat_axis=0)  69.3 us
    all_to_all x2, blocking collectives, exchange(): return lax.all_to_all(blocks, axes, split_axis=0, concat_axis=0)  49.1 us
    all_to_all x3, starting transfers between devices, exchange(): return lax.all_to_all(blocks, axes, split_axis=0, concat_axis=0)  33.1 us
    ppermute x3, starting transfers between devices, swap(): return lax.ppermute(value, axis, [(0, 1), (1, 0)])  15.9 us
    all_gather x1, waiting for transfers between devices, per_device(): feats = lax.all_gather(pair, 'z', axis=0, tiled=True)  10.4 us
    ppermute x3, waiting for transfers between devices, swap(): return lax.ppermute(value, axis, [(0, 1), (1, 0)])  10.4 us
    pallas_call x1, Pallas kernels, project(): pl.pallas_call(project_kernel, grid=(total // TILE,), in_specs=[pl.BlockS...  9.88 us
    pallas_call x1, Pallas kernels, backward(): pl.pallas_call(functools.partial(backward_kernel, features_out=features_o...  9.76 us
  transfers between devices with their start and end apart: 7, of which 7 were waited for; matrix products, arithmetic and copies ran while one was open for 3% of the time, Pallas kernels for 2%

profile of v2, /device:TPU:1, one launch (start us, length us, event | category | flops | bytes accessed | tf_op | source)
XLA Modules:
  0.0 242.6 jit_solution(5862117384699171131)
XLA Ops:
  7.2 0.0 slice-start
  7.2 0.0 all-gather.2.cloned.1.call-start
  7.2 8.4 %collective-permute-start = (bf16[112,1024]{1,0:T(8,128)(2,1)}, bf16[112,1024]{1,0:T(8,128)(2,1)S(1)}, u32[]{:S(2)}, u32[]{:S(2)}) collective-permute-start(bf16[112,1024]{1,0:T(8,128)(2,1)} %param.6), channel_id=1, source_target_pairs={{0,1},{1,0},{2,3},{3,2},{4,5},{5,4},{6,7},{7,6},{8,9},{9,8},{10,11... | collective-permute-start | bytes 688136 | tf_op jit(solution)/shard_map/ppermute | solution.py:25
  15.6 0.0 copy-start.2
  15.6 0.0 slice-done
  15.7 1.3 copy.30
  17.0 0.0 slice-start.1
  17.0 0.0 copy-start.4
  17.0 7.1 %collective-permute-done = bf16[112,1024]{1,0:T(8,128)(2,1)S(1)} collective-permute-done((bf16[112,1024]{1,0:T(8,128)(2,1)}, bf16[112,1024]{1,0:T(8,128)(2,1)S(1)}, u32[]{:S(2)}, u32[]{:S(2)}) %collective-permute-start) | collective-permute-done | bytes 229408 | tf_op jit(solution)/shard_map/ppermute | solution.py:25
  24.1 0.0 copy-done.2
  24.1 0.9 maximum_select_fusion
  25.0 0.0 all-gather.2.cloned.1.call-update
  25.0 0.0 slice-done.1
  25.0 0.2 copy.28
  25.2 0.0 copy-done.4
  25.3 0.1 maximum_bitcast_fusion
  25.3 0.4 copy.22
  25.7 28.8 %all_to_all.25 = bf16[16,40,512]{2,1,0:T(8,128)(2,1)S(1)} all-to-all(bf16[16,40,512]{2,1,0:T(8,128)(2,1)S(1)} %copy.22), channel_id=1, replica_groups=mesh['x'=4,'yl'=4,'c'=2,'z'=8,'yh'=2] {'z','yh'}, dimensions={0} | all-to-all | bytes 1310720 | tf_op jit(solution)/shard_map/all_to_all | solution.py:29
  54.5 12.9 %all-to-all-start.1 = ((bf16[16,96,512]{2,1,0:T(8,128)(2,1)}), bf16[16,96,512]{2,1,0:T(8,128)(2,1)S(1)}, u32[]{:S(2)}, u32[]{:S(2)}) async-start(bf16[16,96,512]{2,1,0:T(8,128)(2,1)} %bitcast.24), calls=%async_computation.1 | async-start | bytes 3145728 | tf_op jit(solution)/shard_map/all_to_all | solution.py:29
  67.4 1.3 dynamic_slice.3
  68.8 1.2 add.149
  70.0 2.2 add_select_fusion.2.index_ref
  72.3 40.8 %all-to-all-done.1 = bf16[16,96,512]{2,1,0:T(8,128)(2,1)S(1)} async-done(((bf16[16,96,512]{2,1,0:T(8,128)(2,1)}), bf16[16,96,512]{2,1,0:T(8,128)(2,1)S(1)}, u32[]{:S(2)}, u32[]{:S(2)}) %all-to-all-start.1) | async-done | bytes 1572896 | tf_op jit(solution)/shard_map/all_to_all | solution.py:29
  113.1 5.7 %pick.1.picked_ref = bf16[1792,512]{1,0:T(8,128)(2,1)S(1)} custom-call(s32[1792,1]{1,0:T(8,128)S(1)} %add_select_fusion.2.index_ref, bf16[640,512]{1,0:T(8,128)(2,1)S(1)} %bitcast.23, bf16[1536,512]{1,0:T(8,128)(2,1)S(1)} %bitcast.22), custom_call_target="tpu_custom_call" | custom-call | flops 3992977408 | bytes 6291456 | tf_op jit(solution)/shard_map/pick/pallas_call | solution.py:55
  118.8 0.0 copy-start
  118.8 1.3 copy-done
  120.1 10.4 %all-gather.2.cloned.1.call-done.feats_ref = bf16[1792,1024]{1,0:T(8,128)(2,1)} async-done(((bf16[224,1024]{1,0:T(8,128)(2,1)}), bf16[1792,1024]{1,0:T(8,128)(2,1)}) %all-gather.2.cloned.1.call-update) | async-done | bytes 3670032 | tf_op jit(solution)/shard_map/all_gather | solution.py:278
  130.6 9.9 %project.1 = (bf16[1792,512]{1,0:T(8,128)(2,1)}, f32[1792,512]{1,0:T(8,128)}, f32[32,128]{1,0:T(8,128)}) custom-call(bf16[1792,1024]{1,0:T(8,128)(2,1)} %all-gather.2.cloned.1.call-done.feats_ref, bf16[1024,512]{1,0:T(8,128)(2,1)} %weight_ref.1, f32[1,512]{1,0:T(1,128)} %bitcast.30, f32[1,512]{1,0:T(1,128)} %bitcast.28, bf16[1792,512]{1,0:T(8,128)(2,1)} %copy-done), custom_call_target="tpu_custom_call" | custom-call | flops 1879048192 | bytes 10485760 | tf_op jit(solution)/shard_map/project/pallas_call | solution.py:103
  140.5 1.4 broadcast_in_dim.31
  141.9 12.7 %all-to-all-start.2 = ((f32[16,32,128]{2,1,0:T(8,128)}), f32[16,32,128]{2,1,0:T(8,128)S(1)}, u32[]{:S(2)}, u32[]{:S(2)}) async-start(f32[16,32,128]{2,1,0:T(8,128)} %broadcast_in_dim.31), calls=%async_computation.2 | async-start | bytes 524288 | tf_op jit(solution)/shard_map/all_to_all | solution.py:29
  154.6 12.8 %all-to-all-done.2.stats_ref = f32[16,32,128]{2,1,0:T(8,128)S(1)} async-done(((f32[16,32,128]{2,1,0:T(8,128)}), f32[16,32,128]{2,1,0:T(8,128)S(1)}, u32[]{:S(2)}, u32[]{:S(2)}) %all-to-all-start.2) | async-done | bytes 262176 | tf_op jit(solution)/shard_map/all_to_all | solution.py:29
  167.3 0.0 copy-start.1
  167.3 0.7 copy-done.1
  168.0 9.8 %backward.1 = (bf16[2056,128]{1,0:T(8,128)(2,1)}, f32[2048,128]{1,0:T(8,128)}, f32[4,128]{1,0:T(4,128)}) custom-call(s32[1]{0:T(128)} %bitcast.core_ref, bf16[1792,1024]{1,0:T(8,128)(2,1)} %all-gather.2.cloned.1.call-done.feats_ref, f32[1,512]{1,0:T(1,128)} %bitcast.29, bf16[1792,512]{1,0:T(8,128)(2,1)} %copy-done, ...), custom_call_target="tpu_custom_call" | custom-call | flops 1879048192 | bytes 10485760 | tf_op jit(solution)/shard_map/backward/pallas_call | solution.py:191
  177.8 0.0 copy-start.3
  177.8 3.8 %collective-permute-start.1 = (bf16[2056,128]{1,0:T(8,128)(2,1)}, bf16[2056,128]{1,0:T(8,128)(2,1)S(1)}, u32[]{:S(2)}, u32[]{:S(2)}) collective-permute-start(bf16[2056,128]{1,0:T(8,128)(2,1)} %get-tuple-element.18), channel_id=1, source_target_pairs={{0,16},{16,0},{1,17},{17,1},{2,18},{18,2},{3,19},{19,3},{4,20},{20... | collective-permute-start | bytes 1579016 | tf_op jit(solution)/shard_map/ppermute | solution.py:25
  181.6 1.7 collective-permute-done.1
  183.3 2.1 add_convert_fusion
  185.4 7.6 %all-to-all-start.3 = ((bf16[16,128,128]{2,1,0:T(8,128)(2,1)}), bf16[16,128,128]{2,1,0:T(8,128)(2,1)S(1)}, u32[]{:S(2)}, u32[]{:S(2)}) async-start(bf16[16,128,128]{2,1,0:T(8,128)(2,1)} %bitcast.9), calls=%async_computation.3 | async-start | bytes 1048576 | tf_op jit(solution)/shard_map/all_to_all | solution.py:29
  193.0 0.0 copy-done.3
  193.0 15.7 %all-to-all-done.3 = bf16[16,128,128]{2,1,0:T(8,128)(2,1)S(1)} async-done(((bf16[16,128,128]{2,1,0:T(8,128)(2,1)}), bf16[16,128,128]{2,1,0:T(8,128)(2,1)S(1)}, u32[]{:S(2)}, u32[]{:S(2)}) %all-to-all-start.3) | async-done | bytes 524320 | tf_op jit(solution)/shard_map/all_to_all | solution.py:29
  208.8 0.1 reduce_sum.12
  208.9 0.1 broadcast_in_dim.32
  209.0 20.4 %all_to_all.26.mine_ref = bf16[16,136,128]{2,1,0:T(8,128)(2,1)S(1)} all-to-all(bf16[16,136,128]{2,1,0:T(8,128)(2,1)S(1)} %broadcast_in_dim.32), channel_id=1, replica_groups=mesh['x'=4,'yl'=4,'c'=2,'z'=8,'yh'=2] {'x','yl'}, dimensions={0} | all-to-all | bytes 1114112 | tf_op jit(solution)/shard_map/all_to_all | solution.py:29
  229.3 3.7 %collective-permute-start.2 = (bf16[16,136,128]{2,1,0:T(8,128)(2,1)S(1)}, bf16[16,136,128]{2,1,0:T(8,128)(2,1)S(1)}, u32[]{:S(2)}, u32[]{:S(2)}) collective-permute-start(bf16[16,136,128]{2,1,0:T(8,128)(2,1)S(1)} %all_to_all.26.mine_ref), channel_id=1, source_target_pairs={{0,16},{16,0},{1,17},{17,1},{2,18},{18,2},{3,19},{19,3},{4,20},{20... | collective-permute-start | bytes 1671176 | tf_op jit(solution)/shard_map/ppermute | solution.py:25
  233.1 1.6 collective-permute-done.2.theirs_ref
  234.6 1.2 assemble.1
  (7 shorter events, 0.1 us)
Async XLA Ops:
  7.2 8.5 %slice-start = ((bf16[128,8192]{1,0:T(8,128)(2,1)}), bf16[96,8192]{1,0:T(8,128)(2,1)S(1)}, s32[]{:S(2)}) async-start(bf16[128,8192]{1,0:T(8,128)(2,1)} %param.11), calls=%async_computation.6 | async-start | bytes 3145728 | tf_op jit(solution)/shard_map/slice | solution.py:277
  7.2 123.4 %all-gather.2.cloned.1.call-start = ((), (), s32[]{:S(2)}) async-start(), calls=%async_computation.5 | async-start | bytes 4128768 | tf_op jit(solution)/shard_map/all_gather | solution.py:278
  7.2 16.9 %collective-permute-start = (bf16[112,1024]{1,0:T(8,128)(2,1)}, bf16[112,1024]{1,0:T(8,128)(2,1)S(1)}, u32[]{:S(2)}, u32[]{:S(2)}) collective-permute-start(bf16[112,1024]{1,0:T(8,128)(2,1)} %param.6), channel_id=1, source_target_pairs={{0,1},{1,0},{2,3},{3,2},{4,5},{5,4},{6,7},{7,6},{8,9},{9,8},{10,11... | collective-permute-start | bytes 688136 | tf_op jit(solution)/shard_map/ppermute | solution.py:25
  15.6 8.5 %copy-start.2 = (bf16[112,1024]{1,0:T(8,128)(2,1)S(1)}, bf16[112,1024]{1,0:T(8,128)(2,1)}, u32[]{:S(2)}) copy-start(bf16[112,1024]{1,0:T(8,128)(2,1)} %param.6) | copy-start | bytes 688132
  17.0 8.0 %slice-start.1 = ((bf16[128,8192]{1,0:T(8,128)(2,1)}), bf16[32,8192]{1,0:T(8,128)(2,1)S(1)}, s32[]{:S(2)}) async-start(bf16[128,8192]{1,0:T(8,128)(2,1)} %param.11), calls=%async_computation.7 | async-start | bytes 1048576 | tf_op jit(solution)/shard_map/slice | solution.py:273
  17.0 8.2 %copy-start.4 = (s32[112]{0:T(128)S(1)}, s32[112]{0:T(128)}, u32[]{:S(2)}) copy-start(s32[112]{0:T(128)} %param.7) | copy-start | bytes 1348
  54.5 58.6 %all-to-all-start.1 = ((bf16[16,96,512]{2,1,0:T(8,128)(2,1)}), bf16[16,96,512]{2,1,0:T(8,128)(2,1)S(1)}, u32[]{:S(2)}, u32[]{:S(2)}) async-start(bf16[16,96,512]{2,1,0:T(8,128)(2,1)} %bitcast.24), calls=%async_computation.1 | async-start | bytes 3145728 | tf_op jit(solution)/shard_map/all_to_all | solution.py:29
  118.8 1.3 copy-start
  141.9 25.4 %all-to-all-start.2 = ((f32[16,32,128]{2,1,0:T(8,128)}), f32[16,32,128]{2,1,0:T(8,128)S(1)}, u32[]{:S(2)}, u32[]{:S(2)}) async-start(f32[16,32,128]{2,1,0:T(8,128)} %broadcast_in_dim.31), calls=%async_computation.2 | async-start | bytes 524288 | tf_op jit(solution)/shard_map/all_to_all | solution.py:29
  167.3 0.7 copy-start.1
  177.8 15.2 %copy-start.3 = (f32[4,128]{1,0:T(4,128)S(1)}, f32[4,128]{1,0:T(4,128)}, u32[]{:S(2)}) copy-start(f32[4,128]{1,0:T(4,128)} %get-tuple-element.19) | copy-start | bytes 6148
  177.8 5.5 %collective-permute-start.1 = (bf16[2056,128]{1,0:T(8,128)(2,1)}, bf16[2056,128]{1,0:T(8,128)(2,1)S(1)}, u32[]{:S(2)}, u32[]{:S(2)}) collective-permute-start(bf16[2056,128]{1,0:T(8,128)(2,1)} %get-tuple-element.18), channel_id=1, source_target_pairs={{0,16},{16,0},{1,17},{17,1},{2,18},{18,2},{3,19},{19,3},{4,20},{20... | collective-permute-start | bytes 1579016 | tf_op jit(solution)/shard_map/ppermute | solution.py:25
  185.4 23.3 %all-to-all-start.3 = ((bf16[16,128,128]{2,1,0:T(8,128)(2,1)}), bf16[16,128,128]{2,1,0:T(8,128)(2,1)S(1)}, u32[]{:S(2)}, u32[]{:S(2)}) async-start(bf16[16,128,128]{2,1,0:T(8,128)(2,1)} %bitcast.9), calls=%async_computation.3 | async-start | bytes 1048576 | tf_op jit(solution)/shard_map/all_to_all | solution.py:29
  229.3 5.3 %collective-permute-start.2 = (bf16[16,136,128]{2,1,0:T(8,128)(2,1)S(1)}, bf16[16,136,128]{2,1,0:T(8,128)(2,1)S(1)}, u32[]{:S(2)}, u32[]{:S(2)}) collective-permute-start(bf16[16,136,128]{2,1,0:T(8,128)(2,1)S(1)} %all_to_all.26.mine_ref), channel_id=1, source_target_pairs={{0,16},{16,0},{1,17},{17,1},{2,18},{18,2},{3,19},{19,3},{4,20},{20... | collective-permute-start | bytes 1671176 | tf_op jit(solution)/shard_map/ppermute | solution.py:25
Sparse Core Ops, SparseCore 0:
  25.1 105.3 all-gather.1

commit v3 on v2

--- a/solution.py
+++ b/solution.py
@@ -15,6 +15,7 @@
 f32 = jnp.float32
 bf16 = jnp.bfloat16
 TILE = 256
+DEEP = 896
 LANES = 128
 EARLY = 32
 HEAD = 8
@@ -70,7 +71,7 @@
     )(index, early, late)
 
 
-def project_kernel(feats_ref, weight_ref, bias_ref, gain_ref, picked_ref, proj_ref, slope_ref, stats_ref):
+def project_kernel(feats_ref, weight_ref, bias_ref, gain_ref, picked_ref, proj_ref, slope_ref, stats_ref, sums):
     step = pl.program_id(0)
     value = jnp.dot(feats_ref[...], weight_ref[...], preferred_element_type=f32) + bias_ref[...]
     cdf = 0.5 * (1.0 + lax.erf(value * 0.7071067811865476))
@@ -84,7 +85,7 @@
 
     @pl.when(step == 0)
     def _():
-        stats_ref[...] = jnp.zeros_like(stats_ref)
+        sums[...] = jnp.zeros_like(sums)
 
     lane = lax.broadcasted_iota(jnp.int32, (LANES, LANES), 1)
     parts = TILE // LANES
@@ -92,11 +93,15 @@
         rows = slice(part * LANES, (part + 1) * LANES)
         both = jnp.where(lane == 0, squares[rows], dots[rows]).T
         row = step * parts + part
-        stats_ref[pl.ds(row, 1), :] = both[0:1]
-        stats_ref[pl.ds(stats_ref.shape[0] // 2 + row, 1), :] = both[1:2]
-
-
-def project(feats, weight, bias, gain, picked):
+        sums[pl.ds(row, 1), :] = both[0:1]
+        sums[pl.ds(sums.shape[0] // 2 + row, 1), :] = both[1:2]
+
+    @pl.when(step == pl.num_programs(0) - 1)
+    def _():
+        stats_ref[...] = jnp.broadcast_to(sums[...][None], stats_ref.shape)
+
+
+def project(feats, weight, bias, gain, picked, copies):
     total, vis = feats.shape
     width = weight.shape[1]
     stat_rows = 2 * (-(-total // LANES // 8) * 8)
@@ -113,14 +118,15 @@
         out_specs=[
             pl.BlockSpec((TILE, width), lambda i: (i, 0)),
             pl.BlockSpec((TILE, width), lambda i: (i, 0)),
-            pl.BlockSpec((stat_rows, LANES), lambda i: (0, 0)),
+            pl.BlockSpec((copies, stat_rows, LANES), lambda i: (0, 0, 0)),
         ],
         out_shape=[
-            jax.ShapeDtypeStruct((total, width), bf16),
-            jax.ShapeDtypeStruct((total, width), f32),
-            jax.ShapeDtypeStruct((stat_rows, LANES), f32),
-        ],
-        compiler_params=params(61),
+            pltpu.HBM((total, width), bf16),
+            pltpu.HBM((total, width), f32),
+            jax.ShapeDtypeStruct((copies, stat_rows, LANES), f32),
+        ],
+        scratch_shapes=[pltpu.VMEM((stat_rows, LANES), f32)],
+        compiler_params=params(24),
         cost_estimate=pl.CostEstimate(flops=2 * total * vis * width, bytes_accessed=10 << 20, transcendentals=total * width),
         name="project",
     )(feats, weight, bias, gain, picked)
@@ -142,7 +148,7 @@
         sums[:half] = inv_rms
         sums[half:] = inv_rms * inv_rms * inv_rms * means[half:]
 
-    parts = TILE // LANES
+    parts = DEEP // LANES
     half = sums.shape[0] // 2
     width = proj_ref.shape[1]
     grads = []
@@ -159,7 +165,7 @@
             columns.append((grad.astype(f32) * slope_ref[rows, cols]).astype(bf16))
         grads.append(jnp.concatenate(columns, axis=1))
     grad_pre = jnp.concatenate(grads, axis=0)
-    bias_acc[...] += jnp.sum(grad_pre.astype(f32).reshape(TILE // 8, 8, width), axis=0)
+    bias_acc[...] += jnp.sum(grad_pre.astype(f32).reshape(DEEP // 8, 8, width), axis=0)
     acc[...] += lax.dot_general(feats_ref[...], grad_pre, (((0,), (0,)), ((), ())), preferred_element_type=f32)
 
     @pl.when(step == pl.num_programs(0) - 1)
@@ -192,13 +198,13 @@
         functools.partial(backward_kernel, features_out=features_out, pieces=pieces),
         grid_spec=pltpu.PrefetchScalarGridSpec(
             num_scalar_prefetch=1,
-            grid=(total // TILE,),
+            grid=(total // DEEP,),
             in_specs=[
-                pl.BlockSpec((TILE, vis), lambda i, c: (i, 0)),
+                pl.BlockSpec((DEEP, vis), lambda i, c: (i, 0)),
                 pl.BlockSpec((1, width), lambda i, c: (0, 0)),
-                pl.BlockSpec((TILE, width), lambda i, c: (i, 0)),
-                pl.BlockSpec((TILE, width), lambda i, c: (i, 0)),
-                pl.BlockSpec((TILE, width), lambda i, c: (i, 0)),
+                pl.BlockSpec((DEEP, width), lambda i, c: (i, 0)),
+                pl.BlockSpec((DEEP, width), lambda i, c: (i, 0)),
+                pl.BlockSpec((DEEP, width), lambda i, c: (i, 0)),
                 pl.BlockSpec(stats.shape, lambda i, c: (0, 0, 0)),
             ],
             out_specs=[
@@ -217,7 +223,7 @@
             jax.ShapeDtypeStruct((out_rows, LANES), f32),
             jax.ShapeDtypeStruct((lines, LANES), f32),
         ],
-        compiler_params=params(61),
+        compiler_params=params(24),
         cost_estimate=pl.CostEstimate(flops=2 * total * vis * width, bytes_accessed=10 << 20, transcendentals=0),
         name="backward",
     )(core, feats, gain, picked, proj, slope, stats)
@@ -274,8 +280,9 @@
     early = exchange(early.transpose(1, 0, 2), MP)
     pair = jnp.concatenate([features, partner], axis=0)
     pair = jnp.where(yh == 0, pair, jnp.concatenate([partner, features], axis=0))
-    pair, late = lax.optimization_barrier((pair, blocks[EARLY:].transpose(1, 0, 2)))
-    feats = lax.all_gather(pair, "z", axis=0, tiled=True)
+    pair, blocks = lax.optimization_barrier((pair, blocks))
+    late = blocks[EARLY:].transpose(1, 0, 2)
+    feats = pltpu.with_memory_space_constraint(lax.all_gather(pair, "z", axis=0, tiled=True), pltpu.HBM)
     late = exchange(late, MP)
 
     digits = early[:, :2, :rows].astype(jnp.int32)
@@ -289,8 +296,9 @@
     picked = pick(index, early.reshape(-1, width), late.reshape(-1, width))
 
     gain = lax.dynamic_slice(norm_gain, (me * width,), (width,))[None]
-    proj, slope, stats = project(feats, proj_weight, proj_bias[None], gain, picked)
-    stats = spread(stats, MP, nm)
+    proj, slope, stats = project(feats, proj_weight, proj_bias[None], gain, picked, nm)
+    stats = exchange(stats, MP)
+    proj, slope = (pltpu.with_memory_space_constraint(value, pltpu.HBM) for value in (proj, slope))
     core = c.astype(jnp.int32)[None]
     sent, kept, bias = backward(core, feats, gain, picked, proj, slope, stats, features_out, chips)
 

time: 244 us -> 240 us (0.984)
  blocking collectives: 49.1 us -> 20.4 us
  starting transfers between devices: 49.1 us -> 64.5 us
  waiting for transfers between devices: 90.2 us -> 99.5 us
  local copies, waits for them, and re-layouts: 7.98 us -> 13 us
  Pallas kernels: 26.5 us -> 22.5 us
    all_to_all x2 -> x1, blocking collectives: 49.1 us -> 20.4 us  [exchange(): return lax.all_to_all(blocks, axes, split_axis=0, concat_axis=0)]
    all_to_all x3 -> x4, starting transfers between devices: 33.1 us -> 48.7 us  [exchange(): return lax.all_to_all(blocks, axes, split_axis=0, concat_axis=0)]
    all_to_all x3 -> x4, waiting for transfers between devices: 69.3 us -> 82.5 us  [exchange(): return lax.all_to_all(blocks, axes, split_axis=0, concat_axis=0)]
    unnamed x11 -> x16, local copies, waits for them, and re-layouts: 2.16 us -> 6.14 us
    pallas_call x1, Pallas kernels: 9.76 us -> 5.96 us  [backward(): pl.pallas_call(functools.partial(backward_kernel, features_out=features_o...]
    all_gather x1, waiting for transfers between devices: 10.4 us -> 7.99 us  [per_device(): lax.all_gather(pair, 'z', axis=0, tiled=True)]
  transfers between devices with their start and end apart: 7 -> 8, of which waited for: 7 -> 8; matrix products, arithmetic and copies ran while one was open for 3% -> 5% of each run, Pallas kernels for 2% -> 2%
where the time goes in v3:
time: 240 us; the launch traced here: 239 us
  waiting for transfers between devices  99.5 us (41%)
  starting transfers between devices  64.5 us (27%)
  Pallas kernels  22.5 us (9%)
  blocking collectives  20.4 us (8%)
  between operations  14.2 us (6%)
  local copies, waits for them, and re-layouts  13 us (5%)
  other arithmetic  5.17 us (2%)
    all_to_all x4, waiting for transfers between devices, exchange(): return lax.all_to_all(blocks, axes, split_axis=0, concat_axis=0)  82.5 us
    all_to_all x4, starting transfers between devices, exchange(): return lax.all_to_all(blocks, axes, split_axis=0, concat_axis=0)  48.7 us
    all_to_all x1, blocking collectives, exchange(): return lax.all_to_all(blocks, axes, split_axis=0, concat_axis=0)  20.4 us
    ppermute x3, starting transfers between devices, swap(): return lax.ppermute(value, axis, [(0, 1), (1, 0)])  15.7 us
    pallas_call x1, Pallas kernels, project(): pl.pallas_call(project_kernel, grid=(total // TILE,), in_specs=[pl.BlockS...  9.58 us
    ppermute x3, waiting for transfers between devices, swap(): return lax.ppermute(value, axis, [(0, 1), (1, 0)])  9.05 us
    all_gather x1, waiting for transfers between devices, per_device(): lax.all_gather(pair, 'z', axis=0, tiled=True)  7.99 us
    unnamed x16, local copies, waits for them, and re-layouts  6.14 us
  transfers between devices with their start and end apart: 8, of which 8 were waited for; matrix products, arithmetic and copies ran while one was open for 5% of the time, Pallas kernels for 2%

profile of v3, /device:TPU:1, one launch (start us, length us, event | category | flops | bytes accessed | tf_op | source)
XLA Modules:
  0.0 239.2 jit_solution(12889414871435047860)
XLA Ops:
  7.2 0.0 all-gather.2.cloned.1.call-start
  7.2 8.3 %collective-permute-start = (bf16[112,1024]{1,0:T(8,128)(2,1)}, bf16[112,1024]{1,0:T(8,128)(2,1)S(1)}, u32[]{:S(2)}, u32[]{:S(2)}) collective-permute-start(bf16[112,1024]{1,0:T(8,128)(2,1)} %param.6), channel_id=1, source_target_pairs={{0,1},{1,0},{2,3},{3,2},{4,5},{5,4},{6,7},{7,6},{8,9},{9,8},{10,11... | collective-permute-start | bytes 688136 | tf_op jit(solution)/shard_map/ppermute | solution.py:26
  15.5 0.0 copy-start.5
  15.5 2.5 %copy.27 = bf16[16,8,16,512]{3,2,1,0:T(8,128)(2,1)S(1)} copy(bf16[16,8,16,512]{3,1,2,0:T(8,128)(2,1)} %bitcast.25) | data formatting | bytes 4194304
  18.0 0.0 copy-start.6
  18.0 6.0 %collective-permute-done = bf16[112,1024]{1,0:T(8,128)(2,1)S(1)} collective-permute-done((bf16[112,1024]{1,0:T(8,128)(2,1)}, bf16[112,1024]{1,0:T(8,128)(2,1)S(1)}, u32[]{:S(2)}, u32[]{:S(2)}) %collective-permute-start) | collective-permute-done | bytes 229408 | tf_op jit(solution)/shard_map/ppermute | solution.py:26
  24.0 0.0 copy-done.5
  24.0 0.9 maximum_select_fusion
  24.9 0.0 all-gather.2.cloned.1.call-update
  24.9 1.1 slice.27
  26.0 0.2 copy.28
  26.1 0.0 copy-done.6
  26.2 0.1 maximum_bitcast_fusion
  26.3 1.2 copy.21
  27.5 13.8 %all-to-all-start = ((bf16[16,40,512]{2,1,0:T(8,128)(2,1)}), bf16[16,40,512]{2,1,0:T(8,128)(2,1)S(1)}, u32[]{:S(2)}, u32[]{:S(2)}) async-start(bf16[16,40,512]{2,1,0:T(8,128)(2,1)} %copy.21), calls=%async_computation | async-start | bytes 1310720 | tf_op jit(solution)/shard_map/all_to_all | solution.py:30
  41.3 1.2 copy.26
  42.5 1.3 slice_bitcast_fusion
  43.8 12.1 %all-to-all-done = bf16[16,40,512]{2,1,0:T(8,128)(2,1)S(1)} async-done(((bf16[16,40,512]{2,1,0:T(8,128)(2,1)}), bf16[16,40,512]{2,1,0:T(8,128)(2,1)S(1)}, u32[]{:S(2)}, u32[]{:S(2)}) %all-to-all-start) | async-done | bytes 655392 | tf_op jit(solution)/shard_map/all_to_all | solution.py:30
  55.9 0.0 copy-start.1
  55.9 14.7 %all-to-all-start.1 = ((bf16[16,96,512]{2,1,0:T(8,128)(2,1)}), bf16[16,96,512]{2,1,0:T(8,128)(2,1)S(1)}, u32[]{:S(2)}, u32[]{:S(2)}) async-start(bf16[16,96,512]{2,1,0:T(8,128)(2,1)} %slice_bitcast_fusion), calls=%async_computation.1 | async-start | bytes 3145728 | tf_op jit(solution)/shard_map/all_to_all | solution.py:30
  70.7 0.8 dynamic_slice.3
  71.5 1.2 add.149
  72.8 3.1 %add_select_fusion.2.index_ref = s32[1792,1]{1,0:T(8,128)} fusion(s32[1792,1]{1,0:T(8,128)} %add.149), kind=kLoop, calls=%fused_computation.7 | loop fusion | flops 50176 | bytes 14336 | tf_op jit(solution)/shard_map/jit(_where)/select_n | solution.py:291
  75.9 0.0 copy-done.1
  75.9 41.9 %all-to-all-done.1 = bf16[16,96,512]{2,1,0:T(8,128)(2,1)S(1)} async-done(((bf16[16,96,512]{2,1,0:T(8,128)(2,1)}), bf16[16,96,512]{2,1,0:T(8,128)(2,1)S(1)}, u32[]{:S(2)}, u32[]{:S(2)}) %all-to-all-start.1) | async-done | bytes 1572896 | tf_op jit(solution)/shard_map/all_to_all | solution.py:30
  117.8 0.0 copy-start
  117.8 1.2 copy-done
  118.9 0.0 copy-start.2
  118.9 1.1 copy-done.2
  120.0 0.0 copy-start.4
  120.0 5.8 %pick.1.picked_ref = bf16[1792,512]{1,0:T(8,128)(2,1)S(1)} custom-call(s32[1792,1]{1,0:T(8,128)S(1)} %copy-done, bf16[640,512]{1,0:T(8,128)(2,1)S(1)} %bitcast.20, bf16[1536,512]{1,0:T(8,128)(2,1)S(1)} %bitcast.19), custom_call_target="tpu_custom_call" | custom-call | flops 3992977408 | bytes 6291456 | tf_op jit(solution)/shard_map/pick/pallas_call | solution.py:56
  125.8 8.0 %all-gather.2.cloned.1.call-done.feats_ref = bf16[1792,1024]{1,0:T(8,128)(2,1)} async-done(((bf16[224,1024]{1,0:T(8,128)(2,1)}), bf16[1792,1024]{1,0:T(8,128)(2,1)}) %all-gather.2.cloned.1.call-update) | async-done | bytes 3670032 | tf_op jit(solution)/shard_map/all_gather | solution.py:285
  133.8 0.0 copy-done.4
  133.8 0.0 copy-start.3
  133.8 1.2 copy-done.3
  135.0 9.6 %project.1 = (bf16[1792,512]{1,0:T(8,128)(2,1)}, f32[1792,512]{1,0:T(8,128)}, f32[16,32,128]{2,1,0:T(8,128)}) custom-call(bf16[1792,1024]{1,0:T(8,128)(2,1)} %all-gather.2.cloned.1.call-done.feats_ref, bf16[1024,512]{1,0:T(8,128)(2,1)S(1)} %copy-done.3, f32[1,512]{1,0:T(1,128)S(1)} %bitcast.23, f32[1,512]{1,0:T(1,128)S(1)} %bitcast.21, ...), custom_call_target="tpu_custom_call" | custom-call | flops 1879048192 | bytes 10485760 | tf_op jit(solution)/shard_map/project/pallas_call | solution.py:108
  144.6 7.8 %all-to-all-start.2 = ((f32[16,32,128]{2,1,0:T(8,128)}), f32[16,32,128]{2,1,0:T(8,128)S(1)}, u32[]{:S(2)}, u32[]{:S(2)}) async-start(f32[16,32,128]{2,1,0:T(8,128)} %get-tuple-element.16), calls=%async_computation.2 | async-start | bytes 524288 | tf_op jit(solution)/shard_map/all_to_all | solution.py:30
  152.4 12.7 %all-to-all-done.2.stats_ref = f32[16,32,128]{2,1,0:T(8,128)S(1)} async-done(((f32[16,32,128]{2,1,0:T(8,128)}), f32[16,32,128]{2,1,0:T(8,128)S(1)}, u32[]{:S(2)}, u32[]{:S(2)}) %all-to-all-start.2) | async-done | bytes 262176 | tf_op jit(solution)/shard_map/all_to_all | solution.py:30
  165.1 6.0 %backward.1 = (bf16[2056,128]{1,0:T(8,128)(2,1)S(1)}, f32[2048,128]{1,0:T(8,128)S(1)}, f32[4,128]{1,0:T(4,128)S(1)}) custom-call(s32[1]{0:T(128)} %bitcast.core_ref, bf16[1792,1024]{1,0:T(8,128)(2,1)} %all-gather.2.cloned.1.call-done.feats_ref, f32[1,512]{1,0:T(1,128)S(1)} %bitcast.22, bf16[1792,512]{1,0:T(8,128)(2,1)S(1)} %pick.1.picked_ref, ...), custom_call_target="tpu_custom_call" | custom-call | flops 1879048192 | bytes 10485760 | tf_op jit(solution)/shard_map/backward/pallas_call | solution.py:197
  171.1 3.7 %collective-permute-start.1 = (bf16[2056,128]{1,0:T(8,128)(2,1)S(1)}, bf16[2056,128]{1,0:T(8,128)(2,1)S(1)}, u32[]{:S(2)}, u32[]{:S(2)}) collective-permute-start(bf16[2056,128]{1,0:T(8,128)(2,1)S(1)} %get-tuple-element.18), channel_id=1, source_target_pairs={{0,16},{16,0},{1,17},{17,1},{2,18},{18,2},{3,19},{19,3},{4,20},{20... | collective-permute-start | bytes 1579016 | tf_op jit(solution)/shard_map/ppermute | solution.py:26
  174.8 1.5 collective-permute-done.1
  176.4 0.9 add_convert_fusion
  177.3 12.4 %all-to-all-start.3 = ((bf16[16,128,128]{2,1,0:T(8,128)(2,1)}), bf16[16,128,128]{2,1,0:T(8,128)(2,1)S(1)}, u32[]{:S(2)}, u32[]{:S(2)}) async-start(bf16[16,128,128]{2,1,0:T(8,128)(2,1)} %bitcast.9), calls=%async_computation.3 | async-start | bytes 1048576 | tf_op jit(solution)/shard_map/all_to_all | solution.py:30
  189.6 15.8 %all-to-all-done.3 = bf16[16,128,128]{2,1,0:T(8,128)(2,1)S(1)} async-done(((bf16[16,128,128]{2,1,0:T(8,128)(2,1)}), bf16[16,128,128]{2,1,0:T(8,128)(2,1)S(1)}, u32[]{:S(2)}, u32[]{:S(2)}) %all-to-all-start.3) | async-done | bytes 524320 | tf_op jit(solution)/shard_map/all_to_all | solution.py:30
  205.4 0.1 reduce_sum.12
  205.5 0.1 broadcast_in_dim.25
  205.6 20.4 %all_to_all.25.mine_ref = bf16[16,136,128]{2,1,0:T(8,128)(2,1)S(1)} all-to-all(bf16[16,136,128]{2,1,0:T(8,128)(2,1)S(1)} %broadcast_in_dim.25), channel_id=1, replica_groups=mesh['x'=4,'yl'=4,'c'=2,'z'=8,'yh'=2] {'x','yl'}, dimensions={0} | all-to-all | bytes 1114112 | tf_op jit(solution)/shard_map/all_to_all | solution.py:30
  225.9 3.7 %collective-permute-start.2 = (bf16[16,136,128]{2,1,0:T(8,128)(2,1)S(1)}, bf16[16,136,128]{2,1,0:T(8,128)(2,1)S(1)}, u32[]{:S(2)}, u32[]{:S(2)}) collective-permute-start(bf16[16,136,128]{2,1,0:T(8,128)(2,1)S(1)} %all_to_all.25.mine_ref), channel_id=1, source_target_pairs={{0,16},{16,0},{1,17},{17,1},{2,18},{18,2},{3,19},{19,3},{4,20},{20... | collective-permute-start | bytes 1671176 | tf_op jit(solution)/shard_map/ppermute | solution.py:26
  229.7 1.6 collective-permute-done.2.theirs_ref
  231.2 1.2 assemble.1
  (7 shorter events, 0.1 us)
Async XLA Ops:
  7.2 126.6 %all-gather.2.cloned.1.call-start = ((), (), s32[]{:S(2)}) async-start(), calls=%async_computation.5 | async-start | bytes 4128768 | tf_op jit(solution)/shard_map/all_gather | solution.py:285
  7.2 16.7 %collective-permute-start = (bf16[112,1024]{1,0:T(8,128)(2,1)}, bf16[112,1024]{1,0:T(8,128)(2,1)S(1)}, u32[]{:S(2)}, u32[]{:S(2)}) collective-permute-start(bf16[112,1024]{1,0:T(8,128)(2,1)} %param.6), channel_id=1, source_target_pairs={{0,1},{1,0},{2,3},{3,2},{4,5},{5,4},{6,7},{7,6},{8,9},{9,8},{10,11... | collective-permute-start | bytes 688136 | tf_op jit(solution)/shard_map/ppermute | solution.py:26
  15.5 8.5 %copy-start.5 = (bf16[112,1024]{1,0:T(8,128)(2,1)S(1)}, bf16[112,1024]{1,0:T(8,128)(2,1)}, u32[]{:S(2)}) copy-start(bf16[112,1024]{1,0:T(8,128)(2,1)} %param.6) | copy-start | bytes 688132
  18.0 8.2 %copy-start.6 = (s32[112]{0:T(128)S(1)}, s32[112]{0:T(128)}, u32[]{:S(2)}) copy-start(s32[112]{0:T(128)} %param.7) | copy-start | bytes 1348
  27.5 28.5 %all-to-all-start = ((bf16[16,40,512]{2,1,0:T(8,128)(2,1)}), bf16[16,40,512]{2,1,0:T(8,128)(2,1)S(1)}, u32[]{:S(2)}, u32[]{:S(2)}) async-start(bf16[16,40,512]{2,1,0:T(8,128)(2,1)} %copy.21), calls=%async_computation | async-start | bytes 1310720 | tf_op jit(solution)/shard_map/all_to_all | solution.py:30
  55.9 20.0 %copy-start.1 = (bf16[16,40,512]{2,1,0:T(8,128)(2,1)}, bf16[16,40,512]{2,1,0:T(8,128)(2,1)S(1)}, u32[]{:S(2)}) copy-start(bf16[16,40,512]{2,1,0:T(8,128)(2,1)S(1)} %all-to-all-done) | copy-start | bytes 1966084
  55.9 61.8 %all-to-all-start.1 = ((bf16[16,96,512]{2,1,0:T(8,128)(2,1)}), bf16[16,96,512]{2,1,0:T(8,128)(2,1)S(1)}, u32[]{:S(2)}, u32[]{:S(2)}) async-start(bf16[16,96,512]{2,1,0:T(8,128)(2,1)} %slice_bitcast_fusion), calls=%async_computation.1 | async-start | bytes 3145728 | tf_op jit(solution)/shard_map/all_to_all | solution.py:30
  117.8 1.2 copy-start
  118.9 1.1 copy-start.2
  120.0 13.8 %copy-start.4 = (f32[512]{0:T(512)S(1)}, f32[512]{0:T(512)}, u32[]{:S(2)}) copy-start(f32[512]{0:T(512)} %param.9) | copy-start | bytes 6148
  133.8 1.2 copy-start.3
  144.6 20.5 %all-to-all-start.2 = ((f32[16,32,128]{2,1,0:T(8,128)}), f32[16,32,128]{2,1,0:T(8,128)S(1)}, u32[]{:S(2)}, u32[]{:S(2)}) async-start(f32[16,32,128]{2,1,0:T(8,128)} %get-tuple-element.16), calls=%async_computation.2 | async-start | bytes 524288 | tf_op jit(solution)/shard_map/all_to_all | solution.py:30
  171.1 5.3 %collective-permute-start.1 = (bf16[2056,128]{1,0:T(8,128)(2,1)S(1)}, bf16[2056,128]{1,0:T(8,128)(2,1)S(1)}, u32[]{:S(2)}, u32[]{:S(2)}) collective-permute-start(bf16[2056,128]{1,0:T(8,128)(2,1)S(1)} %get-tuple-element.18), channel_id=1, source_target_pairs={{0,16},{16,0},{1,17},{17,1},{2,18},{18,2},{3,19},{19,3},{4,20},{20... | collective-permute-start | bytes 1579016 | tf_op jit(solution)/shard_map/ppermute | solution.py:26
  177.3 28.1 %all-to-all-start.3 = ((bf16[16,128,128]{2,1,0:T(8,128)(2,1)}), bf16[16,128,128]{2,1,0:T(8,128)(2,1)S(1)}, u32[]{:S(2)}, u32[]{:S(2)}) async-start(bf16[16,128,128]{2,1,0:T(8,128)(2,1)} %bitcast.9), calls=%async_computation.3 | async-start | bytes 1048576 | tf_op jit(solution)/shard_map/all_to_all | solution.py:30
  225.9 5.3 %collective-permute-start.2 = (bf16[16,136,128]{2,1,0:T(8,128)(2,1)S(1)}, bf16[16,136,128]{2,1,0:T(8,128)(2,1)S(1)}, u32[]{:S(2)}, u32[]{:S(2)}) collective-permute-start(bf16[16,136,128]{2,1,0:T(8,128)(2,1)S(1)} %all_to_all.25.mine_ref), channel_id=1, source_target_pairs={{0,16},{16,0},{1,17},{17,1},{2,18},{18,2},{3,19},{19,3},{4,20},{20... | collective-permute-start | bytes 1671176 | tf_op jit(solution)/shard_map/ppermute | solution.py:26
Sparse Core Ops, SparseCore 0:
  25.0 108.7 all-gather.1

commit v4 on v3

--- a/solution.py
+++ b/solution.py
@@ -32,6 +32,10 @@
 
 def spread(block, axes, count):
     return exchange(jnp.broadcast_to(block[None], (count,) + block.shape), axes)
+
+
+def stay(value):
+    return pltpu.with_memory_space_constraint(value, pltpu.HBM)
 
 
 def params(mib):
@@ -121,8 +125,8 @@
             pl.BlockSpec((copies, stat_rows, LANES), lambda i: (0, 0, 0)),
         ],
         out_shape=[
-            pltpu.HBM((total, width), bf16),
-            pltpu.HBM((total, width), f32),
+            jax.ShapeDtypeStruct((total, width), bf16),
+            jax.ShapeDtypeStruct((total, width), f32),
             jax.ShapeDtypeStruct((copies, stat_rows, LANES), f32),
         ],
         scratch_shapes=[pltpu.VMEM((stat_rows, LANES), f32)],
@@ -133,60 +137,51 @@
 
 
 def backward_kernel(
-    core_ref, feats_ref, gain_ref, picked_ref, proj_ref, slope_ref, stats_ref, sent_ref, kept_ref, bias_ref, acc, bias_acc, sums,
+    core_ref, feats_ref, gain_ref, picked_ref, proj_ref, slope_ref, stats_ref, sent_ref, kept_ref, bias_ref, acc, sums,
     *, features_out, pieces
 ):
-    step = pl.program_id(0)
-
-    @pl.when(step == 0)
-    def _():
-        acc[...] = jnp.zeros_like(acc)
-        bias_acc[...] = jnp.zeros_like(bias_acc)
-        means = jnp.sum(stats_ref[...], axis=0) / features_out
-        half = means.shape[0] // 2
-        inv_rms = lax.rsqrt(means[:half] + EPSILON)
-        sums[:half] = inv_rms
-        sums[half:] = inv_rms * inv_rms * inv_rms * means[half:]
-
-    parts = DEEP // LANES
-    half = sums.shape[0] // 2
-    width = proj_ref.shape[1]
-    grads = []
-    for part in range(parts):
-        rows = slice(part * LANES, (part + 1) * LANES)
-        row = step * parts + part
-        inv_rms = jnp.broadcast_to(sums[pl.ds(row, 1), :], (LANES, LANES)).T
-        factor = jnp.broadcast_to(sums[pl.ds(half + row, 1), :], (LANES, LANES)).T
-        columns = []
+    means = jnp.sum(stats_ref[...], axis=0) / features_out
+    half = means.shape[0] // 2
+    inv_rms = lax.rsqrt(means[:half] + EPSILON)
+    sums[:half] = inv_rms
+    sums[half:] = inv_rms * inv_rms * inv_rms * means[half:]
+    vis, width = acc.shape
+    bias = jnp.zeros((8, width), f32)
+    for step in range(feats_ref.shape[0] // DEEP):
+        grads = []
+        for part in range(DEEP // LANES):
+            row = step * (DEEP // LANES) + part
+            rows = slice(row * LANES, (row + 1) * LANES)
+            inv_rms = jnp.broadcast_to(sums[row : row + 1, :], (LANES, LANES)).T
+            factor = jnp.broadcast_to(sums[half + row : half + row + 1, :], (LANES, LANES)).T
+            columns = []
+            for j in range(width // LANES):
+                cols = slice(j * LANES, (j + 1) * LANES)
+                scaled = picked_ref[rows, cols].astype(f32) * gain_ref[:, cols]
+                grad = (inv_rms * scaled - proj_ref[rows, cols].astype(f32) * factor).astype(bf16)
+                columns.append((grad.astype(f32) * slope_ref[rows, cols]).astype(bf16))
+            grads.append(jnp.concatenate(columns, axis=1))
+        grad_pre = jnp.concatenate(grads, axis=0)
+        bias = bias + jnp.sum(grad_pre.astype(f32).reshape(DEEP // 8, 8, width), axis=0)
+        feats = feats_ref[step * DEEP : (step + 1) * DEEP, :]
+        part = lax.dot_general(feats, grad_pre, (((0,), (0,)), ((), ())), preferred_element_type=f32)
+        acc[...] = part if step == 0 else acc[...] + part
+
+    rows = vis // 2 // pieces
+    core = core_ref[0]
+    for piece in range(pieces):
         for j in range(width // LANES):
             cols = slice(j * LANES, (j + 1) * LANES)
-            scaled = picked_ref[rows, cols].astype(f32) * gain_ref[:, cols]
-            grad = (inv_rms * scaled - proj_ref[rows, cols].astype(f32) * factor).astype(bf16)
-            columns.append((grad.astype(f32) * slope_ref[rows, cols]).astype(bf16))
-        grads.append(jnp.concatenate(columns, axis=1))
-    grad_pre = jnp.concatenate(grads, axis=0)
-    bias_acc[...] += jnp.sum(grad_pre.astype(f32).reshape(DEEP // 8, 8, width), axis=0)
-    acc[...] += lax.dot_general(feats_ref[...], grad_pre, (((0,), (0,)), ((), ())), preferred_element_type=f32)
-
-    @pl.when(step == pl.num_programs(0) - 1)
-    def _():
-        vis = acc.shape[0]
-        rows = vis // 2 // pieces
-        core = core_ref[0]
-        for piece in range(pieces):
-            for j in range(width // LANES):
-                cols = slice(j * LANES, (j + 1) * LANES)
-                at = (piece * (width // LANES) + j) * rows
-                mine = pl.multiple_of(core * (vis // 2) + piece * rows, 8)
-                other = pl.multiple_of((1 - core) * (vis // 2) + piece * rows, 8)
-                kept_ref[at : at + rows, :] = acc[pl.ds(mine, rows), cols]
-                sent_ref[at : at + rows, :] = acc[pl.ds(other, rows), cols].astype(bf16)
-        bias = jnp.sum(bias_acc[...], axis=0, keepdims=True)
-        lines = jnp.concatenate([bias[:, j * LANES : (j + 1) * LANES] for j in range(width // LANES)], axis=0)
-        bias_ref[...] = lines
-        high = lines.astype(bf16).astype(f32)
-        both = jnp.concatenate([high, lines - high], axis=0).astype(bf16)
-        sent_ref[sent_ref.shape[0] - 2 * lines.shape[0] :, :] = both
+            at = (piece * (width // LANES) + j) * rows
+            mine = pl.multiple_of(core * (vis // 2) + piece * rows, 8)
+            other = pl.multiple_of((1 - core) * (vis // 2) + piece * rows, 8)
+            kept_ref[at : at + rows, :] = acc[pl.ds(mine, rows), cols]
+            sent_ref[at : at + rows, :] = acc[pl.ds(other, rows), cols].astype(bf16)
+    bias = jnp.sum(bias, axis=0, keepdims=True)
+    lines = jnp.concatenate([bias[:, j * LANES : (j + 1) * LANES] for j in range(width // LANES)], axis=0)
+    bias_ref[...] = lines
+    high = lines.astype(bf16).astype(f32)
+    sent_ref[sent_ref.shape[0] - 2 * lines.shape[0] :, :] = jnp.concatenate([high, lines - high], axis=0).astype(bf16)
 
 
 def backward(core, feats, gain, picked, proj, slope, stats, features_out, pieces):
@@ -194,35 +189,17 @@
     width = proj.shape[1]
     lines = width // LANES
     out_rows = vis // 2 * lines
+    vmem = pl.BlockSpec(memory_space=pltpu.VMEM)
     return pl.pallas_call(
         functools.partial(backward_kernel, features_out=features_out, pieces=pieces),
-        grid_spec=pltpu.PrefetchScalarGridSpec(
-            num_scalar_prefetch=1,
-            grid=(total // DEEP,),
-            in_specs=[
-                pl.BlockSpec((DEEP, vis), lambda i, c: (i, 0)),
-                pl.BlockSpec((1, width), lambda i, c: (0, 0)),
-                pl.BlockSpec((DEEP, width), lambda i, c: (i, 0)),
-                pl.BlockSpec((DEEP, width), lambda i, c: (i, 0)),
-                pl.BlockSpec((DEEP, width), lambda i, c: (i, 0)),
-                pl.BlockSpec(stats.shape, lambda i, c: (0, 0, 0)),
-            ],
-            out_specs=[
-                pl.BlockSpec((out_rows + 2 * lines, LANES), lambda i, c: (0, 0)),
-                pl.BlockSpec((out_rows, LANES), lambda i, c: (0, 0)),
-                pl.BlockSpec((lines, LANES), lambda i, c: (0, 0)),
-            ],
-            scratch_shapes=[
-                pltpu.VMEM((vis, width), f32),
-                pltpu.VMEM((8, width), f32),
-                pltpu.VMEM(stats.shape[1:], f32),
-            ],
-        ),
+        in_specs=[pl.BlockSpec(memory_space=pltpu.SMEM)] + [vmem] * 6,
+        out_specs=[vmem] * 3,
         out_shape=[
             jax.ShapeDtypeStruct((out_rows + 2 * lines, LANES), bf16),
             jax.ShapeDtypeStruct((out_rows, LANES), f32),
             jax.ShapeDtypeStruct((lines, LANES), f32),
         ],
+        scratch_shapes=[pltpu.VMEM((vis, width), f32), pltpu.VMEM(stats.shape[1:], f32)],
         compiler_params=params(24),
         cost_estimate=pl.CostEstimate(flops=2 * total * vis * width, bytes_accessed=10 << 20, transcendentals=0),
         name="backward",
@@ -271,18 +248,21 @@
     seq_rows, features_out = cotangent.shape
     total = rows * nm
     z, yh, c = lax.axis_index("z"), lax.axis_index("yh"), lax.axis_index("c")
-    me = z * 2 + yh
+    me = (z * 2 + yh) * width
+    low_half = yh == 0
+    core = c.astype(jnp.int32)[None]
     partner = swap(features, "yh")
+    row_position, me, low_half, core = lax.optimization_barrier((row_position, me, low_half, core))
     digits = jnp.stack([row_position // LANES, row_position % LANES]).astype(bf16)
     digits = jnp.pad(digits, ((0, HEAD - 2), (0, width - rows)))
     blocks = cotangent.reshape(seq_rows, nm, width)
     early = jnp.concatenate([jnp.broadcast_to(digits[:, None], (HEAD, nm, width)), blocks[:EARLY]], axis=0)
     early = exchange(early.transpose(1, 0, 2), MP)
     pair = jnp.concatenate([features, partner], axis=0)
-    pair = jnp.where(yh == 0, pair, jnp.concatenate([partner, features], axis=0))
+    pair = jnp.where(low_half, pair, jnp.concatenate([partner, features], axis=0))
     pair, blocks = lax.optimization_barrier((pair, blocks))
     late = blocks[EARLY:].transpose(1, 0, 2)
-    feats = pltpu.with_memory_space_constraint(lax.all_gather(pair, "z", axis=0, tiled=True), pltpu.HBM)
+    feats = lax.all_gather(pair, "z", axis=0, tiled=True)
     late = exchange(late, MP)
 
     digits = early[:, :2, :rows].astype(jnp.int32)
@@ -295,11 +275,9 @@
     )
     picked = pick(index, early.reshape(-1, width), late.reshape(-1, width))
 
-    gain = lax.dynamic_slice(norm_gain, (me * width,), (width,))[None]
-    proj, slope, stats = project(feats, proj_weight, proj_bias[None], gain, picked, nm)
+    gain = lax.dynamic_slice(norm_gain, (me,), (width,))[None]
+    proj, slope, stats = project(stay(feats), stay(proj_weight), proj_bias[None], gain, picked, nm)
     stats = exchange(stats, MP)
-    proj, slope = (pltpu.with_memory_space_constraint(value, pltpu.HBM) for value in (proj, slope))
-    core = c.astype(jnp.int32)[None]
     sent, kept, bias = backward(core, feats, gain, picked, proj, slope, stats, features_out, chips)
 
     lines = width // LANES

time: 240 us -> 234 us (0.975)
  blocking collectives: 20.4 us -> 40.7 us
  waiting for transfers between devices: 99.5 us -> 86.8 us
  starting transfers between devices: 64.5 us -> 56.7 us
  Pallas kernels: 22.5 us -> 18.2 us
    all_to_all x1 -> x2, blocking collectives: 20.4 us -> 40.7 us  [exchange(): return lax.all_to_all(blocks, axes, split_axis=0, concat_axis=0)]
    all_to_all x4 -> x3, waiting for transfers between devices: 82.5 us -> 69.7 us  [exchange(): return lax.all_to_all(blocks, axes, split_axis=0, concat_axis=0)]
    all_to_all x4 -> x3, starting transfers between devices: 48.7 us -> 40.9 us  [exchange(): return lax.all_to_all(blocks, axes, split_axis=0, concat_axis=0)]
    pallas_call x1, Pallas kernels: 5.96 us -> 3.05 us  [backward(): pl.pallas_call(functools.partial(backward_kernel, features_out=features_o...]
  transfers between devices with their start and end apart: 8 -> 7, of which waited for: 8 -> 7; matrix products, arithmetic and copies ran while one was open for 5% -> 5% of each run, Pallas kernels for 2% -> 2%
where the time goes in v4:
time: 234 us
  waiting for transfers between devices  86.8 us (37%)
  starting transfers between devices  56.7 us (24%)
  blocking collectives  40.7 us (17%)
  Pallas kernels  18.2 us (8%)
  between operations  14.2 us (6%)
  local copies, waits for them, and re-layouts  11.8 us (5%)
  other arithmetic  5.15 us (2%)
    all_to_all x3, waiting for transfers between devices, exchange(): return lax.all_to_all(blocks, axes, split_axis=0, concat_axis=0)  69.7 us
    all_to_all x3, starting transfers between devices, exchange(): return lax.all_to_all(blocks, axes, split_axis=0, concat_axis=0)  40.9 us
    all_to_all x2, blocking collectives, exchange(): return lax.all_to_all(blocks, axes, split_axis=0, concat_axis=0)  40.7 us
    ppermute x3, starting transfers between devices, swap(): return lax.ppermute(value, axis, [(0, 1), (1, 0)])  15.7 us
    ppermute x3, waiting for transfers between devices, swap(): return lax.ppermute(value, axis, [(0, 1), (1, 0)])  9.05 us
    pallas_call x1, Pallas kernels, project(): pl.pallas_call(project_kernel, grid=(total // TILE,), in_specs=[pl.BlockS...  8.23 us
    all_gather x1, waiting for transfers between devices, per_device(): feats = lax.all_gather(pair, 'z', axis=0, tiled=True)  7.99 us
    pallas_call x1, Pallas kernels, pick(): pl.pallas_call(pick_kernel, grid=(total // TILE,), in_specs=[pl.BlockSpec...  5.76 us
  transfers between devices with their start and end apart: 7, of which 7 were waited for; matrix products, arithmetic and copies ran while one was open for 5% of the time, Pallas kernels for 2%

profile of v4, /device:TPU:1, one launch (start us, length us, event | category | flops | bytes accessed | tf_op | source)
XLA Modules:
  0.0 233.5 jit_solution(2784418468620439108)
XLA Ops:
  7.2 0.0 all-gather.2.cloned.1.call-start
  7.2 8.3 %collective-permute-start = (bf16[112,1024]{1,0:T(8,128)(2,1)}, bf16[112,1024]{1,0:T(8,128)(2,1)S(1)}, u32[]{:S(2)}, u32[]{:S(2)}) collective-permute-start(bf16[112,1024]{1,0:T(8,128)(2,1)} %param.6), channel_id=1, source_target_pairs={{0,1},{1,0},{2,3},{3,2},{4,5},{5,4},{6,7},{7,6},{8,9},{9,8},{10,11... | collective-permute-start | bytes 688136 | tf_op jit(solution)/shard_map/ppermute | solution.py:26
  15.5 0.0 copy-start.5
  15.5 2.5 %copy.27 = bf16[16,8,16,512]{3,2,1,0:T(8,128)(2,1)S(1)} copy(bf16[16,8,16,512]{3,1,2,0:T(8,128)(2,1)} %bitcast.25) | data formatting | bytes 4194304
  18.0 0.0 copy-start.6
  18.0 6.0 %collective-permute-done = bf16[112,1024]{1,0:T(8,128)(2,1)S(1)} collective-permute-done((bf16[112,1024]{1,0:T(8,128)(2,1)}, bf16[112,1024]{1,0:T(8,128)(2,1)S(1)}, u32[]{:S(2)}, u32[]{:S(2)}) %collective-permute-start) | collective-permute-done | bytes 229408 | tf_op jit(solution)/shard_map/ppermute | solution.py:26
  24.0 0.0 copy-done.5
  24.0 0.9 maximum_select_fusion
  24.9 0.0 all-gather.2.cloned.1.call-update
  24.9 1.1 slice.27
  26.0 0.2 copy.28
  26.1 0.0 copy-done.6
  26.2 0.1 maximum_bitcast_fusion
  26.3 1.2 copy.21
  27.5 13.8 %all-to-all-start = ((bf16[16,40,512]{2,1,0:T(8,128)(2,1)}), bf16[16,40,512]{2,1,0:T(8,128)(2,1)S(1)}, u32[]{:S(2)}, u32[]{:S(2)}) async-start(bf16[16,40,512]{2,1,0:T(8,128)(2,1)} %copy.21), calls=%async_computation | async-start | bytes 1310720 | tf_op jit(solution)/shard_map/all_to_all | solution.py:30
  41.3 1.2 copy.26
  42.5 1.3 slice_bitcast_fusion
  43.8 12.1 %all-to-all-done = bf16[16,40,512]{2,1,0:T(8,128)(2,1)S(1)} async-done(((bf16[16,40,512]{2,1,0:T(8,128)(2,1)}), bf16[16,40,512]{2,1,0:T(8,128)(2,1)S(1)}, u32[]{:S(2)}, u32[]{:S(2)}) %all-to-all-start) | async-done | bytes 655392 | tf_op jit(solution)/shard_map/all_to_all | solution.py:30
  55.9 0.0 copy-start.2
  55.9 14.7 %all-to-all-start.1 = ((bf16[16,96,512]{2,1,0:T(8,128)(2,1)}), bf16[16,96,512]{2,1,0:T(8,128)(2,1)S(1)}, u32[]{:S(2)}, u32[]{:S(2)}) async-start(bf16[16,96,512]{2,1,0:T(8,128)(2,1)} %slice_bitcast_fusion), calls=%async_computation.1 | async-start | bytes 3145728 | tf_op jit(solution)/shard_map/all_to_all | solution.py:30
  70.7 0.8 dynamic_slice.3
  71.5 1.2 add.149
  72.8 3.1 %add_select_fusion.2.index_ref = s32[1792,1]{1,0:T(8,128)} fusion(s32[1792,1]{1,0:T(8,128)} %add.149), kind=kLoop, calls=%fused_computation.7 | loop fusion | flops 50176 | bytes 14336 | tf_op jit(solution)/shard_map/jit(_where)/select_n | solution.py:271
  75.9 0.0 copy-done.2
  75.9 41.9 %all-to-all-done.1 = bf16[16,96,512]{2,1,0:T(8,128)(2,1)S(1)} async-done(((bf16[16,96,512]{2,1,0:T(8,128)(2,1)}), bf16[16,96,512]{2,1,0:T(8,128)(2,1)S(1)}, u32[]{:S(2)}, u32[]{:S(2)}) %all-to-all-start.1) | async-done | bytes 1572896 | tf_op jit(solution)/shard_map/all_to_all | solution.py:30
  117.8 0.0 copy-start.1
  117.8 1.2 copy-done.1
  118.9 0.0 copy-start.3
  118.9 1.1 copy-done.3
  120.0 0.0 copy-start.4
  120.0 5.8 %pick.1.picked_ref = bf16[1792,512]{1,0:T(8,128)(2,1)S(1)} custom-call(s32[1792,1]{1,0:T(8,128)S(1)} %copy-done.1, bf16[640,512]{1,0:T(8,128)(2,1)S(1)} %bitcast.20, bf16[1536,512]{1,0:T(8,128)(2,1)S(1)} %bitcast.19), custom_call_target="tpu_custom_call" | custom-call | flops 3992977408 | bytes 6291456 | tf_op jit(solution)/shard_map/pick/pallas_call | solution.py:60
  125.8 8.0 %all-gather.2.cloned.1.call-done.feats_ref = bf16[1792,1024]{1,0:T(8,128)(2,1)} async-done(((bf16[224,1024]{1,0:T(8,128)(2,1)}), bf16[1792,1024]{1,0:T(8,128)(2,1)}) %all-gather.2.cloned.1.call-update) | async-done | bytes 3670032 | tf_op jit(solution)/shard_map/all_gather | solution.py:265
  133.8 0.0 copy-done.4
  133.8 0.0 copy-start
  133.8 8.2 %project.1 = (bf16[1792,512]{1,0:T(8,128)(2,1)S(1)}, f32[1792,512]{1,0:T(8,128)S(1)}, f32[16,32,128]{2,1,0:T(8,128)S(1)}) custom-call(bf16[1792,1024]{1,0:T(8,128)(2,1)} %all-gather.2.cloned.1.call-done.feats_ref, bf16[1024,512]{1,0:T(8,128)(2,1)} %weight_ref.1, f32[1,512]{1,0:T(1,128)S(1)} %bitcast.23, f32[1,512]{1,0:T(1,128)S(1)} %bitcast.21, ...), custom_call_target="tpu_custom_call" | custom-call | flops 1879048192 | bytes 10485760 | tf_op jit(solution)/shard_map/project/pallas_call | solution.py:112
  142.0 20.3 %all_to_all.25.stats_ref = f32[16,32,128]{2,1,0:T(8,128)S(1)} all-to-all(f32[16,32,128]{2,1,0:T(8,128)S(1)} %get-tuple-element.24), channel_id=1, replica_groups=mesh['x'=4,'yl'=4,'c'=2,'z'=8,'yh'=2] {'z','yh'}, dimensions={0} | all-to-all | bytes 524288 | tf_op jit(solution)/shard_map/all_to_all | solution.py:30
  162.3 0.0 copy-done
  162.3 3.1 %backward.1 = (bf16[2056,128]{1,0:T(8,128)(2,1)S(1)}, f32[2048,128]{1,0:T(8,128)S(1)}, f32[4,128]{1,0:T(4,128)S(1)}) custom-call(s32[1]{0:T(128)} %bitcast.core_ref, bf16[1792,1024]{1,0:T(8,128)(2,1)S(1)} %copy-done, f32[1,512]{1,0:T(1,128)S(1)} %bitcast.22, bf16[1792,512]{1,0:T(8,128)(2,1)S(1)} %pick.1.picked_ref, ...), custom_call_target="tpu_custom_call" | custom-call | flops 1879048192 | bytes 10485760 | tf_op jit(solution)/shard_map/backward/pallas_call | solution.py:193
  165.4 3.7 %collective-permute-start.1 = (bf16[2056,128]{1,0:T(8,128)(2,1)S(1)}, bf16[2056,128]{1,0:T(8,128)(2,1)S(1)}, u32[]{:S(2)}, u32[]{:S(2)}) collective-permute-start(bf16[2056,128]{1,0:T(8,128)(2,1)S(1)} %get-tuple-element.26), channel_id=1, source_target_pairs={{0,16},{16,0},{1,17},{17,1},{2,18},{18,2},{3,19},{19,3},{4,20},{20... | collective-permute-start | bytes 1579016 | tf_op jit(solution)/shard_map/ppermute | solution.py:26
  169.1 1.5 collective-permute-done.1
  170.6 0.9 add_convert_fusion
  171.5 12.4 %all-to-all-start.3 = ((bf16[16,128,128]{2,1,0:T(8,128)(2,1)}), bf16[16,128,128]{2,1,0:T(8,128)(2,1)S(1)}, u32[]{:S(2)}, u32[]{:S(2)}) async-start(bf16[16,128,128]{2,1,0:T(8,128)(2,1)} %bitcast.9), calls=%async_computation.3 | async-start | bytes 1048576 | tf_op jit(solution)/shard_map/all_to_all | solution.py:30
  183.9 15.8 %all-to-all-done.3 = bf16[16,128,128]{2,1,0:T(8,128)(2,1)S(1)} async-done(((bf16[16,128,128]{2,1,0:T(8,128)(2,1)}), bf16[16,128,128]{2,1,0:T(8,128)(2,1)S(1)}, u32[]{:S(2)}, u32[]{:S(2)}) %all-to-all-start.3) | async-done | bytes 524320 | tf_op jit(solution)/shard_map/all_to_all | solution.py:30
  199.7 0.1 reduce_sum.12
  199.8 0.1 broadcast_in_dim.25
  199.9 20.4 %all_to_all.26.mine_ref = bf16[16,136,128]{2,1,0:T(8,128)(2,1)S(1)} all-to-all(bf16[16,136,128]{2,1,0:T(8,128)(2,1)S(1)} %broadcast_in_dim.25), channel_id=1, replica_groups=mesh['x'=4,'yl'=4,'c'=2,'z'=8,'yh'=2] {'x','yl'}, dimensions={0} | all-to-all | bytes 1114112 | tf_op jit(solution)/shard_map/all_to_all | solution.py:30
  220.2 3.7 %collective-permute-start.2 = (bf16[16,136,128]{2,1,0:T(8,128)(2,1)S(1)}, bf16[16,136,128]{2,1,0:T(8,128)(2,1)S(1)}, u32[]{:S(2)}, u32[]{:S(2)}) collective-permute-start(bf16[16,136,128]{2,1,0:T(8,128)(2,1)S(1)} %all_to_all.26.mine_ref), channel_id=1, source_target_pairs={{0,16},{16,0},{1,17},{17,1},{2,18},{18,2},{3,19},{19,3},{4,20},{20... | collective-permute-start | bytes 1671176 | tf_op jit(solution)/shard_map/ppermute | solution.py:26
  224.0 1.6 collective-permute-done.2.theirs_ref
  225.5 1.2 assemble.1
  (7 shorter events, 0.1 us)
Async XLA Ops:
  7.2 126.6 %all-gather.2.cloned.1.call-start = ((), (), s32[]{:S(2)}) async-start(), calls=%async_computation.5 | async-start | bytes 4128768 | tf_op jit(solution)/shard_map/all_gather | solution.py:265
  7.2 16.7 %collective-permute-start = (bf16[112,1024]{1,0:T(8,128)(2,1)}, bf16[112,1024]{1,0:T(8,128)(2,1)S(1)}, u32[]{:S(2)}, u32[]{:S(2)}) collective-permute-start(bf16[112,1024]{1,0:T(8,128)(2,1)} %param.6), channel_id=1, source_target_pairs={{0,1},{1,0},{2,3},{3,2},{4,5},{5,4},{6,7},{7,6},{8,9},{9,8},{10,11... | collective-permute-start | bytes 688136 | tf_op jit(solution)/shard_map/ppermute | solution.py:26
  15.5 8.5 %copy-start.5 = (bf16[112,1024]{1,0:T(8,128)(2,1)S(1)}, bf16[112,1024]{1,0:T(8,128)(2,1)}, u32[]{:S(2)}) copy-start(bf16[112,1024]{1,0:T(8,128)(2,1)} %param.6) | copy-start | bytes 688132
  18.0 8.2 %copy-start.6 = (s32[112]{0:T(128)S(1)}, s32[112]{0:T(128)}, u32[]{:S(2)}) copy-start(s32[112]{0:T(128)} %param.7) | copy-start | bytes 1348
  27.5 28.5 %all-to-all-start = ((bf16[16,40,512]{2,1,0:T(8,128)(2,1)}), bf16[16,40,512]{2,1,0:T(8,128)(2,1)S(1)}, u32[]{:S(2)}, u32[]{:S(2)}) async-start(bf16[16,40,512]{2,1,0:T(8,128)(2,1)} %copy.21), calls=%async_computation | async-start | bytes 1310720 | tf_op jit(solution)/shard_map/all_to_all | solution.py:30
  55.9 20.0 %copy-start.2 = (bf16[16,40,512]{2,1,0:T(8,128)(2,1)}, bf16[16,40,512]{2,1,0:T(8,128)(2,1)S(1)}, u32[]{:S(2)}) copy-start(bf16[16,40,512]{2,1,0:T(8,128)(2,1)S(1)} %all-to-all-done) | copy-start | bytes 1966084
  55.9 61.8 %all-to-all-start.1 = ((bf16[16,96,512]{2,1,0:T(8,128)(2,1)}), bf16[16,96,512]{2,1,0:T(8,128)(2,1)S(1)}, u32[]{:S(2)}, u32[]{:S(2)}) async-start(bf16[16,96,512]{2,1,0:T(8,128)(2,1)} %slice_bitcast_fusion), calls=%async_computation.1 | async-start | bytes 3145728 | tf_op jit(solution)/shard_map/all_to_all | solution.py:30
  117.8 1.2 copy-start.1
  118.9 1.1 copy-start.3
  120.0 13.8 %copy-start.4 = (f32[512]{0:T(512)S(1)}, f32[512]{0:T(512)}, u32[]{:S(2)}) copy-start(f32[512]{0:T(512)} %param.9) | copy-start | bytes 6148
  133.8 28.5 %copy-start = (bf16[1792,1024]{1,0:T(8,128)(2,1)S(1)}, bf16[1792,1024]{1,0:T(8,128)(2,1)}, u32[]{:S(2)}) copy-start(bf16[1792,1024]{1,0:T(8,128)(2,1)} %all-gather.2.cloned.1.call-done.feats_ref) | copy-start | bytes 11010052
  165.4 5.2 %collective-permute-start.1 = (bf16[2056,128]{1,0:T(8,128)(2,1)S(1)}, bf16[2056,128]{1,0:T(8,128)(2,1)S(1)}, u32[]{:S(2)}, u32[]{:S(2)}) collective-permute-start(bf16[2056,128]{1,0:T(8,128)(2,1)S(1)} %get-tuple-element.26), channel_id=1, source_target_pairs={{0,16},{16,0},{1,17},{17,1},{2,18},{18,2},{3,19},{19,3},{4,20},{20... | collective-permute-start | bytes 1579016 | tf_op jit(solution)/shard_map/ppermute | solution.py:26
  171.5 28.1 %all-to-all-start.3 = ((bf16[16,128,128]{2,1,0:T(8,128)(2,1)}), bf16[16,128,128]{2,1,0:T(8,128)(2,1)S(1)}, u32[]{:S(2)}, u32[]{:S(2)}) async-start(bf16[16,128,128]{2,1,0:T(8,128)(2,1)} %bitcast.9), calls=%async_computation.3 | async-start | bytes 1048576 | tf_op jit(solution)/shard_map/all_to_all | solution.py:30
  220.2 5.3 %collective-permute-start.2 = (bf16[16,136,128]{2,1,0:T(8,128)(2,1)S(1)}, bf16[16,136,128]{2,1,0:T(8,128)(2,1)S(1)}, u32[]{:S(2)}, u32[]{:S(2)}) collective-permute-start(bf16[16,136,128]{2,1,0:T(8,128)(2,1)S(1)} %all_to_all.26.mine_ref), channel_id=1, source_target_pairs={{0,16},{16,0},{1,17},{17,1},{2,18},{18,2},{3,19},{19,3},{4,20},{20... | collective-permute-start | bytes 1671176 | tf_op jit(solution)/shard_map/ppermute | solution.py:26
Sparse Core Ops, SparseCore 0:
  25.0 108.7 all-gather.1
